TPU v7x, 768 devices: a whole 4x8x12 slice. The times are simulated.
768 devices in a mesh: dom: 192 (over y, z, core), grp: 4 (over x).
Axes of the slice: x: 4, y: 8, z: 12, core: 2. Of those that a mesh axis runs over, the one named last changes fastest.
Arguments:
- positions: float32 [3, 98304], P(None, ('dom', 'grp')), may hold values from 0 to 1
- features: bfloat16 [128, 98304], P(None, ('dom', 'grp')), may hold values from -6 to 6
- neighbour_weight: bfloat16 [128, 128], replicated, may hold values from -0.5 to 0.5
- adjoint: bfloat16 [256, 98304], P(None, ('dom', 'grp')), may hold values from -0.119628906 to 0.119628906
- basis_weight: bfloat16 [8, 128], replicated, may hold values from -2 to 2
- edge_weight: bfloat16 [128, 64], replicated, may hold values from -0.5 to 0.5
- tile_center: int32 [3072], P(('dom', 'grp')), may hold values from 0 to 3
- tile_neighbour: int32 [3072], P(('dom', 'grp')), may hold values from 0 to 11, as said below
- tile_count: int32 [768], P(('dom', 'grp')), may hold values from 2 to 4, as said below
Outputs:
- position_grad: float32 [3, 98304], P(None, ('dom', 'grp'))
Inputs may be any that keep to these rules, and one draw needn't show every extreme that they name: `tile_count`: some device has all 4 slots live in every draw. `tile_neighbour`: the first slot of every device with an even index s names a block of the lower domain, that of every odd device a block of the upper domain; other slots are uniform over the three domains.
All inputs are finite; a program needn't handle non-finite values.
Results may differ from a plain program's by a relative error of at most 0.0012.
Values may be sent and summed in bfloat16 or wider, within the bound.
A program may use at most 32 MiB of HBM per device.

v0:
```python
import jax
import jax.numpy as jnp
from jax import lax
from jax.sharding import PartitionSpec as P

BLK = 128


slab_length = 1.0
cutoff_square = 4.0


def with_halo(cells, sides, width):
    for axis, dim in sides:
        count = lax.axis_size(axis)
        head = lax.slice_in_dim(cells, 0, width, axis=dim)
        tail = lax.slice_in_dim(cells, cells.shape[dim] - width, cells.shape[dim], axis=dim)
        cells = jnp.concatenate(
            [
                lax.ppermute(tail, axis, [(i, (i + 1) % count) for i in range(count)]),
                cells,
                lax.ppermute(head, axis, [((i + 1) % count, i) for i in range(count)]),
            ],
            axis=dim,
        )
    return cells


def laid_out(pieces, dim):
    lengths = list(pieces.shape[1:])
    lengths[dim] *= pieces.shape[0]
    return jnp.moveaxis(pieces, 0, dim).reshape(lengths)


def gather_packed(arrays, axis, dims):
    line = jnp.concatenate([a.reshape(-1) for a in arrays])
    lines, at, done = (lax.all_gather(line, axis), 0, [])
    for a, dim in zip(arrays, dims):
        pieces = lines[:, at : at + a.size].reshape(-1, *a.shape)
        done.append(laid_out(pieces, dim))
        at += a.size
    return tuple(done)


def from_everyone(value, axis):
    copies = jnp.broadcast_to(value, (lax.axis_size(axis), *value.shape))
    return lax.all_to_all(copies, axis, split_axis=0, concat_axis=0, tiled=True)


def collect(value, axis, dim):
    return laid_out(from_everyone(value, axis), dim)


def cut_along(value, dim, count):
    lengths = value.shape
    pieces = value.reshape(*lengths[:dim], count, lengths[dim] // count, *lengths[dim + 1 :])
    return jnp.moveaxis(pieces, dim, 0)


def sum_at_owner(value, axis, dim):
    count = lax.axis_size(axis)
    pieces = lax.all_to_all(cut_along(value, dim, count), axis, 0, 0, tiled=True)
    return jnp.sum(pieces, axis=0)


def from_behind(value, axis, by):
    count = lax.axis_size(axis)
    return lax.ppermute(value, axis, [(i, (i + by) % count) for i in range(count)])


def decay_rates(basis_count):
    return 0.3 * 1.5 ** jnp.arange(basis_count, dtype=jnp.float32)


def tile_terms(
    center_pos, neigh_pos, center_feat, neigh_feat, adj_center, basis_weight, edge_weight, self_pair
):
    block_size = center_pos.shape[1]
    latent = center_feat.shape[0]
    channels = edge_weight.shape[1]
    basis_count = basis_weight.shape[0]
    displace = neigh_pos[:, None, :] - center_pos[:, :, None]
    dist_sq = jnp.sum(displace * displace, axis=0)
    identity = jnp.eye(block_size, dtype=jnp.float32)
    keep_mask = 1.0 - self_pair * identity
    inner_part = jnp.maximum(1.0 - dist_sq / cutoff_square, 0.0)
    envelope = inner_part * inner_part * keep_mask
    basis_rates = decay_rates(basis_count)
    basis_vals = jnp.exp(-dist_sq[:, :, None] * basis_rates)
    basis_low = basis_vals.astype(jnp.bfloat16)
    pre_act = jnp.dot(
        basis_low.reshape(-1, basis_count), basis_weight, preferred_element_type=jnp.float32
    ).reshape(block_size, block_size, latent)
    pre_act = (
        pre_act
        + center_feat.T.astype(jnp.float32)[:, None, :]
        + neigh_feat.T.astype(jnp.float32)[None, :, :]
    )
    sigmoid_pre = jax.nn.sigmoid(pre_act)
    hidden = (pre_act * sigmoid_pre).astype(jnp.bfloat16)
    weights = jnp.dot(
        hidden.reshape(-1, latent), edge_weight, preferred_element_type=jnp.float32
    ).reshape(block_size, block_size, channels)
    harmonics = jnp.concatenate(
        [jnp.ones((1, block_size, block_size), jnp.float32), displace * 0.5], axis=0
    )
    adj_full = adj_center.astype(jnp.float32).reshape(4, channels, block_size)
    projected = jnp.einsum("mci,mij->ijc", adj_full, harmonics)
    gate_grad = (envelope[:, :, None] * projected).astype(jnp.bfloat16)
    along_chan = jnp.einsum("mci,ijc->mij", adj_full, weights)
    harm_grad = envelope[None] * along_chan
    env_grad = jnp.sum(along_chan * harmonics, axis=0)
    hidden_grad = lax.dot_general(
        gate_grad.reshape(-1, channels),
        edge_weight,
        (((1,), (1,)), ((), ())),
        preferred_element_type=jnp.float32,
    ).reshape(block_size, block_size, latent)
    pre_grad = (hidden_grad * sigmoid_pre * (1.0 + pre_act * (1.0 - sigmoid_pre))).astype(
        jnp.bfloat16
    )
    basis_grad = lax.dot_general(
        pre_grad.reshape(-1, latent),
        basis_weight,
        (((1,), (1,)), ((), ())),
        preferred_element_type=jnp.float32,
    ).reshape(block_size, block_size, basis_count)
    sq_grad = (
        jnp.sum(basis_grad * basis_vals * -basis_rates, axis=2)
        - env_grad * keep_mask * 2.0 * inner_part / cutoff_square
    )
    disp_grad = 2.0 * sq_grad[None] * displace + 0.5 * harm_grad[1:]
    return (-jnp.sum(disp_grad, axis=2), jnp.sum(disp_grad, axis=1))


def on_device(
    positions,
    features,
    neighbour_weight,
    adjoint,
    basis_weight,
    edge_weight,
    tile_center,
    tile_neighbour,
    tile_count,
):
    groups = lax.axis_size("grp")
    own_atoms = positions.shape[1]
    latent = features.shape[0]
    group_atoms = groups * own_atoms
    group_blocks = group_atoms // BLK
    neigh_local = lax.dot_general(
        neighbour_weight, features, (((0,), (0,)), ((), ())), preferred_element_type=jnp.float32
    ).astype(jnp.bfloat16)
    neigh_rim = with_halo(neigh_local, (("dom", 1),), own_atoms)
    pos_rim = with_halo(positions, (("dom", 1),), own_atoms)
    neigh_all, feat_group, adj_group = gather_packed(
        (neigh_rim, features, adjoint), "grp", (1, 1, 1)
    )
    pos_all = collect(pos_rim, "grp", 1)
    pos_window = (
        pos_all.reshape(3, groups, 3, own_atoms).transpose(0, 2, 1, 3).reshape(3, 3 * group_atoms)
    )
    neigh_window = (
        neigh_all.reshape(latent, groups, 3, own_atoms)
        .transpose(0, 2, 1, 3)
        .reshape(latent, 3 * group_atoms)
    )
    slab_shift = (jnp.arange(3 * group_atoms, dtype=jnp.int32) // group_atoms - 1).astype(
        jnp.float32
    ) * slab_length
    zero_rows = jnp.zeros_like(slab_shift)
    pos_window = pos_window + jnp.stack([zero_rows, zero_rows, slab_shift])

    def run_tile(tile_slot, grad_total):
        center = tile_center[tile_slot]
        neigh_block = tile_neighbour[tile_slot]
        center_win = (group_blocks + center) * BLK
        center_own = center * BLK
        neigh_start = neigh_block * BLK
        center_pos = lax.dynamic_slice_in_dim(pos_window, center_win, BLK, 1)
        neigh_pos = lax.dynamic_slice_in_dim(pos_window, neigh_start, BLK, 1)
        center_feat = lax.dynamic_slice_in_dim(feat_group, center_own, BLK, 1)
        neigh_feat = lax.dynamic_slice_in_dim(neigh_window, neigh_start, BLK, 1)
        adj_center = lax.dynamic_slice_in_dim(adj_group, center_own, BLK, 1)
        self_pair = (neigh_block == center + group_blocks).astype(jnp.float32)
        center_grad, neigh_grad = tile_terms(
            center_pos,
            neigh_pos,
            center_feat,
            neigh_feat,
            adj_center,
            basis_weight,
            edge_weight,
            self_pair,
        )
        old_center = lax.dynamic_slice_in_dim(grad_total, center_win, BLK, 1)
        grad_total = lax.dynamic_update_slice_in_dim(
            grad_total, old_center + center_grad, center_win, 1
        )
        old_neigh = lax.dynamic_slice_in_dim(grad_total, neigh_start, BLK, 1)
        return lax.dynamic_update_slice_in_dim(grad_total, old_neigh + neigh_grad, neigh_start, 1)

    partial_grad = lax.fori_loop(
        0, tile_count[0], run_tile, jnp.zeros((3, 3 * group_atoms), jnp.float32)
    )
    slabs = partial_grad.reshape(3, 3, group_atoms)
    group_sums = sum_at_owner(slabs, "grp", 2)
    from_upper = from_behind(group_sums[:, 0], "dom", -1)
    from_lower = from_behind(group_sums[:, 2], "dom", 1)
    return group_sums[:, 1] + from_upper + from_lower


def solution(mesh):
    placed = (
        P(None, ("dom", "grp")),
        P(None, ("dom", "grp")),
        P(),
        P(None, ("dom", "grp")),
        P(),
        P(),
        P(("dom", "grp")),
        P(("dom", "grp")),
        P(("dom", "grp")),
    )
    return jax.shard_map(
        on_device, mesh=mesh, in_specs=placed, out_specs=P(None, ("dom", "grp")), check_vma=False
    )
```

profile of v0, /device:TPU:2, one launch (start us, length us, event | category | flops | bytes accessed | tf_op | source)
XLA Modules:
  0.0 178.5 jit_solution(6491064044097380934)
XLA Ops:
  0.0 2.1 %collective-permute-start = (f32[3,128]{1,0:T(4,128)}, f32[3,128]{1,0:T(4,128)S(1)}, u32[]{:S(2)}, u32[]{:S(2)}) collective-permute-start(f32[3,128]{1,0:T(4,128)} %param.11), channel_id=1, source_target_pairs={{0,4},{4,8},{8,12},{12,16},{16,20},{20,24},{24,28},{28,32},{32,36}... | collective-permute-start | bytes 4616 | tf_op jit(solution)/shard_map/ppermute | solution.py:20
  2.1 16.9 %collective-permute-start.1 = (f32[3,128]{1,0:T(4,128)}, f32[3,128]{1,0:T(4,128)S(1)}, u32[]{:S(2)}, u32[]{:S(2)}) collective-permute-start(f32[3,128]{1,0:T(4,128)} %param.11), channel_id=1, source_target_pairs={{4,0},{8,4},{12,8},{16,12},{20,16},{24,20},{28,24},{32,28},{36,32}... | collective-permute-start | bytes 4616 | tf_op jit(solution)/shard_map/ppermute | solution.py:22
  19.0 1.0 convolution_convert_fusion
  20.0 2.6 %collective-permute-start.3 = (bf16[128,128]{0,1:T(8,128)(2,1)S(1)}, bf16[128,128]{0,1:T(8,128)(2,1)S(1)}, u32[]{:S(2)}, u32[]{:S(2)}) collective-permute-start(bf16[128,128]{0,1:T(8,128)(2,1)S(1)} %convolution_convert_fusion), channel_id=1, source_target_pairs={{4,0},{8,4},{12,8},{16,12},{20,16},{24,20},{28,24},{32,28},{36,32}... | collective-permute-start | bytes 98312 | tf_op jit(solution)/shard_map/ppermute | solution.py:22
  22.6 1.9 %collective-permute-start.2 = (bf16[128,128]{0,1:T(8,128)(2,1)S(1)}, bf16[128,128]{0,1:T(8,128)(2,1)S(1)}, u32[]{:S(2)}, u32[]{:S(2)}) collective-permute-start(bf16[128,128]{0,1:T(8,128)(2,1)S(1)} %convolution_convert_fusion), channel_id=1, source_target_pairs={{0,4},{4,8},{8,12},{12,16},{16,20},{20,24},{24,28},{28,32},{32,36}... | collective-permute-start | bytes 98312 | tf_op jit(solution)/shard_map/ppermute | solution.py:20
  25.9 4.8 %all-to-all-start = ((f32[4,3,384]{2,1,0:T(4,128)}), f32[4,3,384]{2,1,0:T(4,128)S(1)}, u32[]{:S(2)}, u32[]{:S(2)}) async-start(f32[4,3,384]{2,1,0:T(4,128)} %broadcast_in_dim.5), calls=%async_computation | async-start | bytes 49152 | tf_op jit(solution)/shard_map/all_to_all | solution.py:47
  30.8 3.8 %all-to-all-done = f32[4,3,384]{2,1,0:T(4,128)S(1)} async-done(((f32[4,3,384]{2,1,0:T(4,128)}), f32[4,3,384]{2,1,0:T(4,128)S(1)}, u32[]{:S(2)}, u32[]{:S(2)}) %all-to-all-start) | async-done | bytes 18464 | tf_op jit(solution)/shard_map/all_to_all | solution.py:47
  34.9 1.2 bitcast_add_fusion
  37.2 13.6 %all-gather = bf16[393216]{0:T(1024)(128)(2,1)S(1)} all-gather(bf16[98304]{0:T(1024)(128)(2,1)S(1)} %pad_maximum_fusion), channel_id=2, replica_groups=mesh['dom'=192,'grp'=4] {'grp'}, dimensions={0}, use_global_device_ids=true | all-gather | bytes 983040 | tf_op jit(solution)/shard_map/all_gather | solution.py:37
  52.2 80.7 %while.10 = (s32[]{:T(128)}, f32[3,1536]{1,0:T(4,128)S(1)}, s32[]{:T(128)}, s32[4]{0:T(128)S(1)}, s32[4]{0:T(128)S(1)}, /*index=5*/f32[3,1536]{0,1:T(8,128)}, bf...) while((s32[]{:T(128)}, f32[3,1536]{1,0:T(4,128)S(1)}, ...), condition=%wide.region_6.7_spmd, body=%wide.region_0.6_spmd.sunk | while | flops 662389120 | bytes 35591812 | solution.py:204
  57.6 0.9 constant_dynamic-slice_fusion.7
  59.7 5.0 %fusion.72 = f32[128,128,128]{2,1,0:T(8,128)} fusion(f32[8]{0:T(128)S(1)} %get-tuple-element.254, f32[128,128]{1,0:T(8,128)S(1)} %get-tuple-element.256, bf16[8,128]{1,0:T(8,128)(2,1)S(1)} %get-tuple-element.309), kind=kOutput, calls=%fused_computation.20.clone.1 | convolution fusion | flops 33816576 | bytes 8456224 | tf_op jit(solution)/shard_map/while/body/dot_general | solution.py:91
  64.7 7.0 %fusion.73 = f32[128,128]{1,0:T(8,128)S(1)} fusion(f32[128,128,128]{2,1,0:T(8,128)} %fusion.72, f32[128,128]{1,0:T(8,128)S(1)} %get-tuple-element.257, f32[128,128]{1,0:T(8,128)S(1)} %get-tuple-element.258, bf16[128,128,64]{1,2,0:T(8,128)(2,1)S(1)} %multiply_convert_fusion.22, f32[8]{0:T(128)S(1)} %get-tuple-element.261, ...), kind=kOutput, calls=%fused_computation.12.clone.1 | convolution fusion | flops 325566464 | bytes 10766400 | tf_op jit(solution)/shard_map/while/body/dot_general | solution.py:122
  71.8 6.7 %multiply_reduce_fusion.2 = (f32[128,128]{1,0:T(8,128)S(1)}, f32[4,128,128]{2,0,1:T(4,128)S(1)}) fusion(f32[3,128,128]{2,0,1:T(4,128)S(1)} %get-tuple-element.253, bf16[4,64,128]{1,0,2:T(4,128)(2,1)S(1)} %copy.122, f32[128,128,128]{2,1,0:T(8,128)} %fusion.72, f32[128,128]{1,0:T(8,128)S(1)} %get-tuple-element.257, ...), kind=kOutput, calls=%fused_computation.23.clone.1 | convolution fusion | flops 291618816 | bytes 9125888 | tf_op jit(solution)/shard_map/while/body/mci,ijc->mij/dot_general | solution.py:110
  86.3 5.0 %fusion.72 = f32[128,128,128]{2,1,0:T(8,128)} fusion(f32[8]{0:T(128)S(1)} %get-tuple-element.254, f32[128,128]{1,0:T(8,128)S(1)} %get-tuple-element.256, bf16[8,128]{1,0:T(8,128)(2,1)S(1)} %get-tuple-element.309), kind=kOutput, calls=%fused_computation.20.clone.1 | convolution fusion | flops 33816576 | bytes 8456224 | tf_op jit(solution)/shard_map/while/body/dot_general | solution.py:91
  91.3 7.0 %fusion.73 = f32[128,128]{1,0:T(8,128)S(1)} fusion(f32[128,128,128]{2,1,0:T(8,128)} %fusion.72, f32[128,128]{1,0:T(8,128)S(1)} %get-tuple-element.257, f32[128,128]{1,0:T(8,128)S(1)} %get-tuple-element.258, bf16[128,128,64]{1,2,0:T(8,128)(2,1)S(1)} %multiply_convert_fusion.22, f32[8]{0:T(128)S(1)} %get-tuple-element.261, ...), kind=kOutput, calls=%fused_computation.12.clone.1 | convolution fusion | flops 325566464 | bytes 10766400 | tf_op jit(solution)/shard_map/while/body/dot_general | solution.py:122
  98.4 6.7 %multiply_reduce_fusion.2 = (f32[128,128]{1,0:T(8,128)S(1)}, f32[4,128,128]{2,0,1:T(4,128)S(1)}) fusion(f32[3,128,128]{2,0,1:T(4,128)S(1)} %get-tuple-element.253, bf16[4,64,128]{1,0,2:T(4,128)(2,1)S(1)} %copy.122, f32[128,128,128]{2,1,0:T(8,128)} %fusion.72, f32[128,128]{1,0:T(8,128)S(1)} %get-tuple-element.257, ...), kind=kOutput, calls=%fused_computation.23.clone.1 | convolution fusion | flops 291618816 | bytes 9125888 | tf_op jit(solution)/shard_map/while/body/mci,ijc->mij/dot_general | solution.py:110
  112.9 5.0 %fusion.72 = f32[128,128,128]{2,1,0:T(8,128)} fusion(f32[8]{0:T(128)S(1)} %get-tuple-element.254, f32[128,128]{1,0:T(8,128)S(1)} %get-tuple-element.256, bf16[8,128]{1,0:T(8,128)(2,1)S(1)} %get-tuple-element.309), kind=kOutput, calls=%fused_computation.20.clone.1 | convolution fusion | flops 33816576 | bytes 8456224 | tf_op jit(solution)/shard_map/while/body/dot_general | solution.py:91
  118.0 7.0 %fusion.73 = f32[128,128]{1,0:T(8,128)S(1)} fusion(f32[128,128,128]{2,1,0:T(8,128)} %fusion.72, f32[128,128]{1,0:T(8,128)S(1)} %get-tuple-element.257, f32[128,128]{1,0:T(8,128)S(1)} %get-tuple-element.258, bf16[128,128,64]{1,2,0:T(8,128)(2,1)S(1)} %multiply_convert_fusion.22, f32[8]{0:T(128)S(1)} %get-tuple-element.261, ...), kind=kOutput, calls=%fused_computation.12.clone.1 | convolution fusion | flops 325566464 | bytes 10766400 | tf_op jit(solution)/shard_map/while/body/dot_general | solution.py:122
  125.0 6.7 %multiply_reduce_fusion.2 = (f32[128,128]{1,0:T(8,128)S(1)}, f32[4,128,128]{2,0,1:T(4,128)S(1)}) fusion(f32[3,128,128]{2,0,1:T(4,128)S(1)} %get-tuple-element.253, bf16[4,64,128]{1,0,2:T(4,128)(2,1)S(1)} %copy.122, f32[128,128,128]{2,1,0:T(8,128)} %fusion.72, f32[128,128]{1,0:T(8,128)S(1)} %get-tuple-element.257, ...), kind=kOutput, calls=%fused_computation.23.clone.1 | convolution fusion | flops 291618816 | bytes 9125888 | tf_op jit(solution)/shard_map/while/body/mci,ijc->mij/dot_general | solution.py:110
  132.9 34.8 %all_to_all.10 = f32[4,3,3,128]{3,2,1,0:T(4,128)S(1)} all-to-all(f32[4,3,3,128]{3,2,1,0:T(4,128)S(1)} %copy.86), channel_id=1, replica_groups=mesh['dom'=192,'grp'=4] {'grp'}, dimensions={0} | all-to-all | bytes 36864 | tf_op jit(solution)/shard_map/all_to_all | solution.py:62
  167.8 1.9 %collective-permute-start.4 = (f32[3,128]{1,0:T(4,128)S(1)}, f32[3,128]{1,0:T(4,128)S(1)}, u32[]{:S(2)}, u32[]{:S(2)}) collective-permute-start(f32[3,128]{1,0:T(4,128)S(1)} %bitcast.124), channel_id=1, source_target_pairs={{0,764},{4,0},{8,4},{12,8},{16,12},{20,16},{24,20},{28,24},{32,28}... | collective-permute-start | bytes 4616 | tf_op jit(solution)/shard_map/ppermute | solution.py:68
  169.7 2.4 %collective-permute-start.5 = (f32[3,128]{1,0:T(4,128)S(1)}, f32[3,128]{1,0:T(4,128)S(1)}, u32[]{:S(2)}, u32[]{:S(2)}) collective-permute-start(f32[3,128]{1,0:T(4,128)S(1)} %bitcast.123), channel_id=1, source_target_pairs={{0,4},{4,8},{8,12},{12,16},{16,20},{20,24},{24,28},{28,32},{32,36}... | collective-permute-start | bytes 4616 | tf_op jit(solution)/shard_map/ppermute | solution.py:68
  172.2 5.8 %collective-permute-done.5 = f32[3,128]{1,0:T(4,128)S(1)} collective-permute-done((f32[3,128]{1,0:T(4,128)S(1)}, f32[3,128]{1,0:T(4,128)S(1)}, u32[]{:S(2)}, u32[]{:S(2)}) %collective-permute-start.5) | collective-permute-done | bytes 1568 | tf_op jit(solution)/shard_map/ppermute | solution.py:68
  (105 shorter events, 16.6 us)
Async XLA Ops:
  0.0 19.0 %copy-start = (bf16[128,128]{1,0:T(8,128)(2,1)S(1)}, bf16[128,128]{1,0:T(8,128)(2,1)}, u32[]{:S(2)}) copy-start(bf16[128,128]{1,0:T(8,128)(2,1)} %param.13) | copy-start | bytes 98308
  0.0 52.2 %copy-start.6 = (s32[4]{0:T(128)S(1)}, s32[4]{0:T(128)}, u32[]{:S(2)}) copy-start(s32[4]{0:T(128)} %param.18) | copy-start | bytes 52
  0.0 52.2 %copy-start.5 = (s32[4]{0:T(128)S(1)}, s32[4]{0:T(128)}, u32[]{:S(2)}) copy-start(s32[4]{0:T(128)} %param.17) | copy-start | bytes 52
  0.0 52.2 %copy-start.4 = (bf16[128,64]{0,1:T(8,128)(2,1)S(1)}, bf16[128,64]{0,1:T(8,128)(2,1)}, u32[]{:S(2)}) copy-start(bf16[128,64]{0,1:T(8,128)(2,1)} %param.16) | copy-start | bytes 49156
  0.0 52.2 %copy-start.3 = (bf16[8,128]{1,0:T(8,128)(2,1)S(1)}, bf16[8,128]{1,0:T(8,128)(2,1)}, u32[]{:S(2)}) copy-start(bf16[8,128]{1,0:T(8,128)(2,1)} %param.15) | copy-start | bytes 6148
  0.0 24.5 %collective-permute-start = (f32[3,128]{1,0:T(4,128)}, f32[3,128]{1,0:T(4,128)S(1)}, u32[]{:S(2)}, u32[]{:S(2)}) collective-permute-start(f32[3,128]{1,0:T(4,128)} %param.11), channel_id=1, source_target_pairs={{0,4},{4,8},{8,12},{12,16},{16,20},{20,24},{24,28},{28,32},{32,36}... | collective-permute-start | bytes 4616 | tf_op jit(solution)/shard_map/ppermute | solution.py:20
  2.1 22.5 %collective-permute-start.1 = (f32[3,128]{1,0:T(4,128)}, f32[3,128]{1,0:T(4,128)S(1)}, u32[]{:S(2)}, u32[]{:S(2)}) collective-permute-start(f32[3,128]{1,0:T(4,128)} %param.11), channel_id=1, source_target_pairs={{4,0},{8,4},{12,8},{16,12},{20,16},{24,20},{28,24},{32,28},{36,32}... | collective-permute-start | bytes 4616 | tf_op jit(solution)/shard_map/ppermute | solution.py:22
  20.0 16.2 %collective-permute-start.3 = (bf16[128,128]{0,1:T(8,128)(2,1)S(1)}, bf16[128,128]{0,1:T(8,128)(2,1)S(1)}, u32[]{:S(2)}, u32[]{:S(2)}) collective-permute-start(bf16[128,128]{0,1:T(8,128)(2,1)S(1)} %convolution_convert_fusion), channel_id=1, source_target_pairs={{4,0},{8,4},{12,8},{16,12},{20,16},{24,20},{28,24},{32,28},{36,32}... | collective-permute-start | bytes 98312 | tf_op jit(solution)/shard_map/ppermute | solution.py:22
  22.6 13.6 %collective-permute-start.2 = (bf16[128,128]{0,1:T(8,128)(2,1)S(1)}, bf16[128,128]{0,1:T(8,128)(2,1)S(1)}, u32[]{:S(2)}, u32[]{:S(2)}) collective-permute-start(bf16[128,128]{0,1:T(8,128)(2,1)S(1)} %convolution_convert_fusion), channel_id=1, source_target_pairs={{0,4},{4,8},{8,12},{12,16},{16,20},{20,24},{24,28},{28,32},{32,36}... | collective-permute-start | bytes 98312 | tf_op jit(solution)/shard_map/ppermute | solution.py:20
  25.9 8.8 %all-to-all-start = ((f32[4,3,384]{2,1,0:T(4,128)}), f32[4,3,384]{2,1,0:T(4,128)S(1)}, u32[]{:S(2)}, u32[]{:S(2)}) async-start(f32[4,3,384]{2,1,0:T(4,128)} %broadcast_in_dim.5), calls=%async_computation | async-start | bytes 49152 | tf_op jit(solution)/shard_map/all_to_all | solution.py:47
  53.0 5.8 %copy-start.1 = (bf16[128,1536]{0,1:T(8,128)(2,1)}, bf16[128,1536]{0,1:T(8,128)(2,1)S(1)}, u32[]{:S(2)}) copy-start(bf16[128,1536]{0,1:T(8,128)(2,1)S(1)} %get-tuple-element.311) | copy-start | bytes 1179652 | tf_op jit(solution)/shard_map/while
  71.8 7.2 %copy-start.2 = (bf16[128,1536]{0,1:T(8,128)(2,1)S(1)}, bf16[128,1536]{0,1:T(8,128)(2,1)}, u32[]{:S(2)}) copy-start(bf16[128,1536]{0,1:T(8,128)(2,1)} %copy-done.1) | copy-start | bytes 1179652 | tf_op jit(solution)/shard_map/while
  79.7 5.8 %copy-start.1 = (bf16[128,1536]{0,1:T(8,128)(2,1)}, bf16[128,1536]{0,1:T(8,128)(2,1)S(1)}, u32[]{:S(2)}) copy-start(bf16[128,1536]{0,1:T(8,128)(2,1)S(1)} %get-tuple-element.311) | copy-start | bytes 1179652 | tf_op jit(solution)/shard_map/while
  98.4 7.2 %copy-start.2 = (bf16[128,1536]{0,1:T(8,128)(2,1)S(1)}, bf16[128,1536]{0,1:T(8,128)(2,1)}, u32[]{:S(2)}) copy-start(bf16[128,1536]{0,1:T(8,128)(2,1)} %copy-done.1) | copy-start | bytes 1179652 | tf_op jit(solution)/shard_map/while
  106.3 5.8 %copy-start.1 = (bf16[128,1536]{0,1:T(8,128)(2,1)}, bf16[128,1536]{0,1:T(8,128)(2,1)S(1)}, u32[]{:S(2)}) copy-start(bf16[128,1536]{0,1:T(8,128)(2,1)S(1)} %get-tuple-element.311) | copy-start | bytes 1179652 | tf_op jit(solution)/shard_map/while
  125.0 7.2 %copy-start.2 = (bf16[128,1536]{0,1:T(8,128)(2,1)S(1)}, bf16[128,1536]{0,1:T(8,128)(2,1)}, u32[]{:S(2)}) copy-start(bf16[128,1536]{0,1:T(8,128)(2,1)} %copy-done.1) | copy-start | bytes 1179652 | tf_op jit(solution)/shard_map/while
  167.8 4.3 %collective-permute-start.4 = (f32[3,128]{1,0:T(4,128)S(1)}, f32[3,128]{1,0:T(4,128)S(1)}, u32[]{:S(2)}, u32[]{:S(2)}) collective-permute-start(f32[3,128]{1,0:T(4,128)S(1)} %bitcast.124), channel_id=1, source_target_pairs={{0,764},{4,0},{8,4},{12,8},{16,12},{20,16},{24,20},{28,24},{32,28}... | collective-permute-start | bytes 4616 | tf_op jit(solution)/shard_map/ppermute | solution.py:68
  169.7 8.2 %collective-permute-start.5 = (f32[3,128]{1,0:T(4,128)S(1)}, f32[3,128]{1,0:T(4,128)S(1)}, u32[]{:S(2)}, u32[]{:S(2)}) collective-permute-start(f32[3,128]{1,0:T(4,128)S(1)} %bitcast.123), channel_id=1, source_target_pairs={{0,4},{4,8},{8,12},{12,16},{16,20},{20,24},{24,28},{28,32},{32,36}... | collective-permute-start | bytes 4616 | tf_op jit(solution)/shard_map/ppermute | solution.py:68
where the time goes:
time: 180 us; the launch traced here: 179 us
  matrix products  59.7 us (33%)
  blocking collectives  48.5 us (27%)
  starting transfers between devices  32.6 us (18%)
  loops' own time  11.6 us (6%)
  local copies, waits for them, and re-layouts  10.5 us (6%)
  waiting for transfers between devices  9.65 us (5%)
  other arithmetic  5.8 us (3%)
    all_to_all x1, blocking collectives, sum_at_owner(): lax.all_to_all(cut_along(value, dim, count), axis, 0, 0, tiled=True)  34.8 us
    dot_general x3, matrix products, tile_terms(): lax.dot_general(pre_grad.reshape(-1, latent), basis_weight, (((1,), (1,))...  21.1 us
    dot_general x3, matrix products, tile_terms(): along_chan = jnp.einsum('mci,ijc->mij', adj_full, weights)  20.1 us
    ppermute x2, starting transfers between devices, with_halo(): lax.ppermute(head, axis, [((i + 1) % count, i) for i in range(count)])  19.5 us
    dot_general x3, matrix products, tile_terms(): jnp.dot(basis_low.reshape(-1, basis_count), basis_weight, preferred_eleme...  15.1 us
    all_gather x1, blocking collectives, gather_packed(): lines, at, done = (lax.all_gather(line, axis), 0, [])  13.6 us
    another operation x1, loops' own time, on_device(): lax.fori_loop(0, tile_count[0], run_tile, jnp.zeros((3, 3 * group_atoms),...  11.6 us
    ppermute x2, waiting for transfers between devices, from_behind(): lax.ppermute(value, axis, [(i, (i + by) % count) for i in range(count)])  5.8 us
  transfers between devices with their start and end apart: 7, of which 2 were waited for; matrix products, arithmetic and copies ran while one was open for 2% of the time, Pallas kernels for 0%

commit v1 on v0

v1 whole, which is shorter than its diff:
```python
import jax
import jax.numpy as jnp
from jax import lax
from jax.experimental import pallas as pl
from jax.experimental.pallas import tpu as pltpu
from jax.sharding import PartitionSpec as P

BF = jnp.bfloat16
F32 = jnp.float32
BLK = 128
GRP = 4
SLOTS = 4
NSLOT = GRP * SLOTS
QTR = BLK // GRP
PAIRS = QTR // 2
U = PAIRS // 2
MESH = pl.DeviceIdType.MESH

RATES = tuple(0.3 * 1.5**b for b in range(8))


def pair_values(h, hg):
    one = jnp.asarray(1.0, BF)
    t = jnp.tanh(h)
    p = one + t
    hid = h * p
    return hid, hg * (p + hid * (one - t))


def body(
    pos_in, feat_in, nw_in, adj_in, bw_in, ew_in, tc_in, tn_in, cnt_in, out_ref,
    featx, posx, meta, meta_sm, at_send, at_all, res_send, res_recv,
    nf, ptr, cposb, bt32, bt, lhs, wred, rhs, bas, al, pr, ds, y_s, s2_s, nacc, cacc,
    hb, xb,
    fx_send, fz_send, f_recv, a_send, a_recv, p_send, p_recv, m_send, m_recv,
    r_send, r_recv, loc_sem,
):
    g = lax.axis_index("grp")
    dm = lax.axis_index("dom")
    n_dom = lax.axis_size("dom")
    up = lax.rem(dm + 1, n_dom)
    dn = lax.rem(dm + n_dom - 1, n_dom)
    xs = [lax.rem(g + j, GRP) for j in range(1, GRP)]
    barrier = pltpu.get_barrier_semaphore()
    for x in xs:
        pl.semaphore_signal(barrier, inc=1, device_id=(dm, x), device_id_type=MESH)
    for d in (up, dn):
        for x in range(GRP):
            pl.semaphore_signal(barrier, inc=1, device_id=(d, x), device_id_type=MESH)

    lane8 = lax.broadcasted_iota(jnp.int32, (8, BLK), 1)
    sub8 = lax.broadcasted_iota(jnp.int32, (8, BLK), 0)
    mv = jnp.zeros((8, BLK), jnp.int32)
    for t in range(SLOTS):
        mv = jnp.where(lane8 == t, tc_in[t], mv)
        mv = jnp.where(lane8 == SLOTS + t, tn_in[t], mv)
    meta[g] = jnp.where(lane8 == 2 * SLOTS, cnt_in[0], mv)
    posx[GRP + g] = jnp.concatenate([pos_in[...], jnp.zeros((5, BLK), F32)], 0)
    at_send[...] = adj_in[...].astype(F32).T.astype(BF)

    pl.semaphore_wait(barrier, 11)

    def rcopy(src, dst, ss, rs, dev):
        return pltpu.make_async_remote_copy(
            src_ref=src, dst_ref=dst, send_sem=ss, recv_sem=rs, device_id=dev, device_id_type=MESH
        )

    sends = []

    def go(c):
        c.start()
        sends.append(c)

    own = GRP + g
    for j, x in enumerate(xs):
        go(rcopy(posx.at[own], posx.at[own], p_send.at[j], p_recv.at[own], (dm, x)))
        go(rcopy(meta.at[g], meta.at[g], m_send.at[j], m_recv.at[g], (dm, x)))
    for x in range(GRP):
        go(rcopy(posx.at[own], posx.at[g], p_send.at[3 + x], p_recv.at[g], (up, x)))
        go(rcopy(posx.at[own], posx.at[2 * GRP + g], p_send.at[7 + x], p_recv.at[2 * GRP + g], (dn, x)))
    for j, x in enumerate(xs):
        rows = pl.ds(pl.multiple_of(QTR * x, QTR), QTR)
        go(rcopy(at_send.at[rows, :], at_all.at[g], a_send.at[j], a_recv.at[g], (dm, x)))
    for j, x in enumerate((xs[0], xs[2], xs[1])):
        go(rcopy(feat_in, featx.at[own], fx_send.at[j], f_recv.at[own], (dm, x)))
    go(rcopy(feat_in, featx.at[g], fz_send.at[0], f_recv.at[g], (up, g)))
    go(rcopy(feat_in, featx.at[2 * GRP + g], fz_send.at[1], f_recv.at[2 * GRP + g], (dn, g)))

    featx[own] = feat_in[...]
    at_all[g] = at_send[pl.ds(pl.multiple_of(QTR * g, QTR), QTR), :]
    wred[...] = jnp.concatenate(
        [
            jnp.concatenate([jnp.zeros((8, BLK), F32), bw_in[...].astype(F32)], 1),
            jnp.zeros((8, 2 * BLK), F32),
        ],
        0,
    ).astype(BF)
    nacc[...] = jnp.zeros_like(nacc)
    cacc[...] = jnp.zeros_like(cacc)

    for x in xs:
        rcopy(at_all.at[x], at_all.at[x], a_send.at[0], a_recv.at[x], (dm, x)).wait_recv()
    at2 = at_all[...].reshape(BLK, 4 * 64)
    for m in range(4):
        bm = lax.dot_general(
            at2[:, 64 * m : 64 * m + 64], ew_in[...], (((1,), (1,)), ((), ())), preferred_element_type=F32
        )
        hi = bm.astype(BF).astype(F32)
        bt32[pl.ds(m, BLK, stride=8), :] = hi
        bt32[pl.ds(4 + m, BLK, stride=8), :] = bm - hi

    for j, x in enumerate((xs[0], xs[2], xs[1])):
        blk = GRP + x
        rcopy(featx.at[blk], featx.at[blk], fx_send.at[0], f_recv.at[blk], (dm, x)).wait_recv()
        go(rcopy(featx.at[blk], featx.at[x], fz_send.at[2 + 2 * j], f_recv.at[x], (up, g)))
        go(rcopy(featx.at[blk], featx.at[2 * GRP + x], fz_send.at[3 + 2 * j], f_recv.at[2 * GRP + x], (dn, g)))

    lane = lax.broadcasted_iota(jnp.int32, (BLK, BLK), 1)
    wt = (
        jnp.concatenate([bw_in[...].astype(F32), jnp.zeros((BLK - 8, BLK), F32)], 0).T * 0.5
    )
    for c in range(GRP):
        fr = pltpu.roll(featx[GRP + c].astype(F32) * 0.5, lax.rem(8 + BLK - QTR * g, BLK), 1)
        for w in range(2):
            wr = bt32[1024 // 8 * (2 * c + w) : 1024 // 8 * (2 * c + w + 1), :].T
            for r in range(8):
                cp = 16 * c + 8 * w + r
                s = 16 * w + 2 * r
                f2 = pltpu.roll(fr, BLK - s, 1) if s else fr
                lhs[cp, 0:BLK, :] = jnp.where(lane < 8, wt, jnp.where(lane < 16, f2, 0.0)).astype(BF)
                sh = (16 - 16 * r) % BLK
                b2 = pltpu.roll(wr, sh, 1) if sh else wr
                lhs[cp, BLK : 2 * BLK, :] = jnp.where(lane < 16, 0.0, b2).astype(BF)
                bt[cp] = bt32[16 * cp : 16 * cp + 16, :].astype(BF)

    for x in xs:
        rcopy(posx.at[GRP + x], posx.at[GRP + x], p_send.at[0], p_recv.at[GRP + x], (dm, x)).wait_recv()
        rcopy(meta.at[x], meta.at[x], m_send.at[0], m_recv.at[x], (dm, x)).wait_recv()
    for x in range(GRP):
        rcopy(posx.at[x], posx.at[x], p_send.at[0], p_recv.at[x], (dn, x)).wait_recv()
        rcopy(posx.at[2 * GRP + x], posx.at[2 * GRP + x], p_send.at[0], p_recv.at[2 * GRP + x], (up, x)).wait_recv()
    mc = pltpu.make_async_copy(meta, meta_sm, loc_sem)
    mc.start()
    mc.wait()
    pc = jnp.concatenate([posx[GRP + c] for c in range(GRP)] + [jnp.zeros((BLK - 8 * GRP, BLK), F32)], 0)
    ptr[...] = pc.T
    pq = ptr[pl.ds(pl.multiple_of(QTR * g, QTR), QTR), :]
    for c in range(GRP):
        for m in range(3):
            cposb[c, m] = jnp.broadcast_to(pq[:, 8 * c + m : 8 * c + m + 1], (QTR, BLK))

    col = lax.broadcasted_iota(jnp.int32, (8, BLK), 0)
    neg = jnp.zeros((8, BLK), F32)
    for b, rate in enumerate(RATES):
        neg = jnp.where(col == b, -rate, neg)
    half_neg = 0.5 * neg
    z8 = jnp.zeros((8, BLK), F32)
    one0 = jnp.where(sub8 == 0, 1.0, 0.0)
    one1 = jnp.where(sub8 == 1, 1.0, 0.0)

    def slot_of(t):
        gs = t // SLOTS
        ti = lax.rem(t, SLOTS)
        return meta_sm[gs, 0, ti], meta_sm[gs, 0, SLOTS + ti], gs, ti

    def geometry(t, carry):
        c, n, gs, ti = slot_of(t)
        row = posx[n]
        shift = (n // GRP - 1).astype(F32)
        selff = jnp.where(n == c + GRP, 1.0, 0.0)
        npos = [jnp.broadcast_to(row[m : m + 1, :], (8, BLK)) for m in range(3)]
        npos[2] = npos[2] + shift
        for q in range(QTR // 8):
            sl = slice(8 * q, 8 * q + 8)
            d = [npos[m] - cposb[c, m, sl, :] for m in range(3)]
            s2 = d[0] * d[0] + d[1] * d[1] + d[2] * d[2]
            keep = 1.0 - jnp.where(lane8 == sub8 + (QTR * g + 8 * q), selff, 0.0)
            inner = jnp.maximum(1.0 - s2 * 0.25, 0.0)
            env = inner * inner * keep
            s2_s[sl, :] = s2
            hd = [v * 0.5 for v in d]
            ys = [env] + [env * v for v in hd]
            for m in range(4):
                y_s[pl.ds(64 * q + m, 8, stride=8), :] = ys[m]
                y_s[pl.ds(64 * q + m + 4, 8, stride=8), :] = ys[m]
            for k, v in enumerate(hd + [env, inner * keep]):
                ds[t, k, sl, :] = v
        for r in range(PAIRS):
            p = t * PAIRS + r
            bs = []
            for e in range(2):
                b = jnp.exp(s2_s[pl.ds(2 * r + e, 8, stride=0), :] * neg)
                bas[2 * p + e] = b * half_neg
                bs.append(b)
            y0 = y_s[16 * r : 16 * r + 8, :]
            y1 = y_s[16 * r + 8 : 16 * r + 16, :]
            top = jnp.concatenate([jnp.concatenate([bs[0], one0], 0), jnp.concatenate([bs[1], one1], 0)], 1)
            low = jnp.concatenate([jnp.concatenate([y0, z8], 0), jnp.concatenate([z8, y1], 0)], 1)
            rhs[p, 0:16, :] = top.astype(BF)
            rhs[p, 16:32, :] = low.astype(BF)
        return carry

    lax.fori_loop(0, NSLOT, geometry, 0)

    def project(b):
        v = lax.dot_general(nw_in[...], featx[b], (((0,), (0,)), ((), ())), preferred_element_type=F32)
        nf[b] = v.astype(BF).astype(F32) * 0.5

    for c in range(GRP):
        project(GRP + c)
    for x in [g, *xs]:
        rcopy(featx.at[x], featx.at[x], fz_send.at[0], f_recv.at[x], (dn, g)).wait_recv()
        project(x)
        rcopy(featx.at[2 * GRP + x], featx.at[2 * GRP + x], fz_send.at[0], f_recv.at[2 * GRP + x], (up, g)).wait_recv()
        project(2 * GRP + x)

    zpad = jnp.zeros((96, 2 * BLK), BF)
    zbt = jnp.zeros((16, BLK), BF)

    def stage_a(c, n, r, p, buf):
        o = jnp.dot(lhs[c * PAIRS + r], jnp.concatenate([rhs[p], zpad], 0), preferred_element_type=F32)
        nn = nf[n]
        hb[buf, 0:BLK, :] = (o[:BLK] + jnp.concatenate([nn, nn], 1)).astype(BF)
        hb[buf, BLK : 2 * BLK, :] = o[BLK:].astype(BF)

    def stage_b(buf):
        for k in range(0, BLK, 16):
            hid, pg = pair_values(hb[buf, k : k + 16, :], hb[buf, BLK + k : BLK + k + 16, :])
            xb[buf, k : k + 16, :] = hid
            xb[buf, BLK + k : BLK + k + 16, :] = pg

    def stage_c(c, r, p, buf):
        lr = jnp.concatenate([jnp.concatenate([bt[c * PAIRS + r], zbt], 1), wred[...]], 0)
        o = jnp.dot(lr, xb[buf], preferred_element_type=F32)
        for e in range(2):
            cut = slice(BLK * e, BLK * e + BLK)
            al[2 * p + e] = o[8 * e : 8 * e + 8, cut]
            pr[2 * p + e] = o[16:24, cut] * bas[2 * p + e]

    def main(k, carry):
        ta = jnp.minimum(k, NSLOT - 1)
        tl = jnp.maximum(k - 1, 0)
        ca, na, _, _ = slot_of(ta)
        cl, _, _, _ = slot_of(tl)
        for half in range(2):
            for u in range(U):
                r = half * U + u
                stage_a(ca, na, r, ta * PAIRS + r, r)
                stage_b((1 - half) * U + u)
                stage_c(cl, r, tl * PAIRS + r, r)
        return carry

    lax.fori_loop(0, NSLOT + 1, main, 0)

    def finish(t, carry):
        c, n, gs, ti = slot_of(t)
        live = jnp.where(ti < meta_sm[gs, 0, 2 * SLOTS], 1.0, 0.0)
        ng = [jnp.zeros((8, BLK), F32)] * 3
        base = t * QTR
        for q in range(QTR // 8):
            sl = slice(8 * q, 8 * q + 8)
            at8 = pl.ds(base + 8 * q, 8)
            s = pr[at8, 0, :]
            for b in range(1, 8):
                s = s + pr[at8, b, :]
            av = [al[at8, m, :] + al[at8, m + 4, :] for m in range(4)]
            hd = [ds[t, k, sl, :] for k in range(3)]
            env = ds[t, 3, sl, :]
            ik = ds[t, 4, sl, :]
            eg = av[0] + av[1] * hd[0] + av[2] * hd[1] + av[3] * hd[2]
            sq = (s - 0.5 * eg * ik) * (4.0 * live)
            ev = env * (0.5 * live)
            for m in range(3):
                dg = sq * hd[m] + ev * av[m + 1]
                ng[m] = ng[m] + dg
                for k in range(GRP):
                    cacc[k, m, sl, :] += jnp.where(c == k, 1.0, 0.0) * dg
        v = jnp.concatenate([jnp.sum(a, axis=0, keepdims=True) for a in ng] + [jnp.zeros((5, BLK), F32)], 0)
        for k in range(3 * GRP):
            nacc[k] += jnp.where(n == k, 1.0, 0.0) * v
        return carry

    lax.fori_loop(0, NSLOT, finish, 0)

    crow = jnp.concatenate(
        [jnp.sum(cacc[:, m].reshape(BLK, BLK).T, axis=0, keepdims=True) for m in range(3)]
        + [jnp.zeros((5, BLK), F32)],
        0,
    )
    mine = (lane8 >= QTR * g) & (lane8 < QTR * g + QTR)
    for x in range(GRP):
        moved = pltpu.roll(crow, lax.rem(QTR * g + BLK - QTR * x, BLK), 1)
        res_send[x] = nacc[x]
        res_send[GRP + x] = nacc[GRP + x] - jnp.where(mine, moved, 0.0)
        res_send[2 * GRP + x] = nacc[2 * GRP + x]
    for j, x in enumerate(xs):
        go(rcopy(res_send.at[GRP + x], res_recv.at[own], r_send.at[j], r_recv.at[own], (dm, x)))
    for x in range(GRP):
        go(rcopy(res_send.at[x], res_recv.at[2 * GRP + g], r_send.at[3 + x], r_recv.at[2 * GRP + g], (dn, x)))
        go(rcopy(res_send.at[2 * GRP + x], res_recv.at[g], r_send.at[7 + x], r_recv.at[g], (up, x)))
    total = res_send[own]
    for x in xs:
        rcopy(res_recv.at[GRP + x], res_recv.at[GRP + x], r_send.at[0], r_recv.at[GRP + x], (dm, x)).wait_recv()
        total = total + res_recv[GRP + x]
    for x in range(GRP):
        rcopy(res_recv.at[x], res_recv.at[x], r_send.at[0], r_recv.at[x], (dn, x)).wait_recv()
        total = total + res_recv[x]
        rcopy(
            res_recv.at[2 * GRP + x], res_recv.at[2 * GRP + x], r_send.at[0], r_recv.at[2 * GRP + x], (up, x)
        ).wait_recv()
        total = total + res_recv[2 * GRP + x]
    out_ref[...] = total[0:3, :]
    for c in sends:
        c.wait_send()


def on_device(*args):
    V = pltpu.VMEM
    vs = pl.BlockSpec(memory_space=pltpu.VMEM)
    sm = pl.BlockSpec(memory_space=pltpu.SMEM)
    D = pltpu.SemaphoreType.DMA
    return pl.pallas_call(
        body,
        out_shape=jax.ShapeDtypeStruct((3, BLK), F32),
        in_specs=[vs] * 6 + [sm] * 3,
        out_specs=vs,
        scratch_shapes=[
            V((3 * GRP, BLK, BLK), BF),
            V((3 * GRP, 8, BLK), F32),
            V((GRP, 8, BLK), jnp.int32),
            pltpu.SMEM((GRP, 8, BLK), jnp.int32),
            V((BLK, 256), BF),
            V((GRP, QTR, 256), BF),
            V((3 * GRP, 8, BLK), F32),
            V((3 * GRP, 8, BLK), F32),
            V((3 * GRP, BLK, BLK), F32),
            V((BLK, BLK), F32),
            V((GRP, 3, QTR, BLK), F32),
            V((8 * BLK, BLK), F32),
            V((GRP * PAIRS, 16, BLK), BF),
            V((GRP * PAIRS, 2 * BLK, BLK), BF),
            V((16, 2 * BLK), BF),
            V((NSLOT * PAIRS, 32, 2 * BLK), BF),
            V((NSLOT * QTR, 8, BLK), F32),
            V((NSLOT * QTR, 8, BLK), F32),
            V((NSLOT * QTR, 8, BLK), F32),
            V((NSLOT, 5, QTR, BLK), F32),
            V((8 * QTR, BLK), F32),
            V((QTR, BLK), F32),
            V((3 * GRP, 8, BLK), F32),
            V((GRP, 3, QTR, BLK), F32),
            V((2 * U, 2 * BLK, 2 * BLK), BF),
            V((2 * U, 2 * BLK, 2 * BLK), BF),
            D((3,)),
            D((8,)),
            D((12,)),
            D((3,)),
            D((4,)),
            D((11,)),
            D((12,)),
            D((3,)),
            D((4,)),
            D((11,)),
            D((12,)),
            D,
        ],
        compiler_params=pltpu.CompilerParams(collective_id=0, has_side_effects=True),
        name="allegro_forces",
    )(*args)


def solution(mesh):
    placed = (
        P(None, ("dom", "grp")),
        P(None, ("dom", "grp")),
        P(),
        P(None, ("dom", "grp")),
        P(),
        P(),
        P(("dom", "grp")),
        P(("dom", "grp")),
        P(("dom", "grp")),
    )
    return jax.shard_map(
        on_device, mesh=mesh, in_specs=placed, out_specs=P(None, ("dom", "grp")), check_vma=False
    )
```

time: 180 us -> 55.7 us (0.31)
  the two profiles are of different devices: /device:TPU:2 before, /device:TPU:1 now
where the time goes in v1:
time: 55.7 us; the launch traced here: 55.4 us
  Pallas kernels  52.1 us (94%)
  local copies, waits for them, and re-layouts  2.65 us (5%)
  between operations  0.66 us (1%)
    pallas_call x1, Pallas kernels, on_device(): pl.pallas_call(body, out_shape=jax.ShapeDtypeStruct((3, BLK), F32), in_sp...  52.1 us
    unnamed x2, local copies, waits for them, and re-layouts  2.65 us

profile of v1, /device:TPU:1, one launch (start us, length us, event | category | flops | bytes accessed | tf_op | source)
XLA Modules:
  0.0 55.4 jit_solution(16608796471050462685)
XLA Ops:
  0.7 1.4 %copy.10.ew_in = bf16[128,64]{1,0:T(8,128)(2,1)} copy(bf16[128,64]{0,1:T(8,128)(2,1)} %param.14) | data formatting | bytes 32768 | tf_op args[5]
  2.1 52.1 %allegro_forces.1 = f32[3,128]{1,0:T(4,128)} custom-call(f32[3,128]{1,0:T(4,128)} %pos_in.1, bf16[128,128]{1,0:T(8,128)(2,1)} %feat_in.1, bf16[128,128]{1,0:T(8,128)(2,1)} %nw_in.1, bf16[256,128]{1,0:T(8,128)(2,1)} %adj_in.1, bf16[8,128]{1,0:T(8,128)(2,1)} %bw_in.1, bf16[128,64]{1,0:T(8,128)(2,1)} %copy.10.ew_in, s32[4]{0:T(128)} %tc_in.1, s32[4]{0:T(128)} %tn_in.1, ...), custom_call_target="tpu_custom_call" | custom-call | tf_op jit(solution)/shard_map/allegro_forces/pallas_call | solution.py:322
  54.2 1.2 %copy.13 = f32[3,128]{1,0:T(4,128)} copy(f32[3,128]{1,0:T(4,128)} %allegro_forces.1) | data formatting | bytes 3072

commit v2 on v1

--- a/solution.py
+++ b/solution.py
@@ -13,7 +13,6 @@
 NSLOT = GRP * SLOTS
 QTR = BLK // GRP
 PAIRS = QTR // 2
-U = PAIRS // 2
 MESH = pl.DeviceIdType.MESH
 
 RATES = tuple(0.3 * 1.5**b for b in range(8))
@@ -30,7 +29,7 @@
 def body(
     pos_in, feat_in, nw_in, adj_in, bw_in, ew_in, tc_in, tn_in, cnt_in, out_ref,
     featx, posx, meta, meta_sm, at_send, at_all, res_send, res_recv,
-    nf, ptr, cposb, bt32, bt, lhs, wred, rhs, bas, al, pr, ds, y_s, s2_s, nacc, cacc,
+    nf, ptr, cposb, bt32, bt, lp, lh, oneh, wred, rhs, bas, al, pr, ds, y_s, s2_s, nacc, cacc,
     hb, xb,
     fx_send, fz_send, f_recv, a_send, a_recv, p_send, p_recv, m_send, m_recv,
     r_send, r_recv, loc_sem,
@@ -103,7 +102,7 @@
     at2 = at_all[...].reshape(BLK, 4 * 64)
     for m in range(4):
         bm = lax.dot_general(
-            at2[:, 64 * m : 64 * m + 64], ew_in[...], (((1,), (1,)), ((), ())), preferred_element_type=F32
+            at2[:, 64 * m : 64 * m + 64], ew_in[...], (((1,), (0,)), ((), ())), preferred_element_type=F32
         )
         hi = bm.astype(BF).astype(F32)
         bt32[pl.ds(m, BLK, stride=8), :] = hi
@@ -120,18 +119,17 @@
         jnp.concatenate([bw_in[...].astype(F32), jnp.zeros((BLK - 8, BLK), F32)], 0).T * 0.5
     )
     for c in range(GRP):
-        fr = pltpu.roll(featx[GRP + c].astype(F32) * 0.5, lax.rem(8 + BLK - QTR * g, BLK), 1)
+        fr = pltpu.roll(featx[GRP + c].astype(F32) * 0.5, lax.rem(16 + BLK - QTR * g, BLK), 1)
         for w in range(2):
-            wr = bt32[1024 // 8 * (2 * c + w) : 1024 // 8 * (2 * c + w + 1), :].T
-            for r in range(8):
-                cp = 16 * c + 8 * w + r
-                s = 16 * w + 2 * r
-                f2 = pltpu.roll(fr, BLK - s, 1) if s else fr
-                lhs[cp, 0:BLK, :] = jnp.where(lane < 8, wt, jnp.where(lane < 16, f2, 0.0)).astype(BF)
-                sh = (16 - 16 * r) % BLK
-                b2 = pltpu.roll(wr, sh, 1) if sh else wr
-                lhs[cp, BLK : 2 * BLK, :] = jnp.where(lane < 16, 0.0, b2).astype(BF)
-                bt[cp] = bt32[16 * cp : 16 * cp + 16, :].astype(BF)
+            f2 = pltpu.roll(fr, BLK - 16, 1) if w else fr
+            lp[2 * c + w] = jnp.where(lane < 8, wt, jnp.where(lane < 16, 0.0, f2)).astype(BF)
+            lh[2 * c + w] = bt32[BLK * (2 * c + w) : BLK * (2 * c + w + 1), :].T.astype(BF)
+    for cp in range(GRP * PAIRS):
+        bt[cp] = bt32[16 * cp : 16 * cp + 16, :].astype(BF)
+    row16 = lax.broadcasted_iota(jnp.int32, (16, 2 * BLK), 0)
+    side = lax.broadcasted_iota(jnp.int32, (16, 2 * BLK), 1) // BLK
+    for r in range(8):
+        oneh[r] = jnp.where(row16 == 2 * r + side, 1.0, 0.0).astype(BF)
 
     for x in xs:
         rcopy(posx.at[GRP + x], posx.at[GRP + x], p_send.at[0], p_recv.at[GRP + x], (dm, x)).wait_recv()
@@ -155,8 +153,6 @@
         neg = jnp.where(col == b, -rate, neg)
     half_neg = 0.5 * neg
     z8 = jnp.zeros((8, BLK), F32)
-    one0 = jnp.where(sub8 == 0, 1.0, 0.0)
-    one1 = jnp.where(sub8 == 1, 1.0, 0.0)
 
     def slot_of(t):
         gs = t // SLOTS
@@ -194,7 +190,7 @@
                 bs.append(b)
             y0 = y_s[16 * r : 16 * r + 8, :]
             y1 = y_s[16 * r + 8 : 16 * r + 16, :]
-            top = jnp.concatenate([jnp.concatenate([bs[0], one0], 0), jnp.concatenate([bs[1], one1], 0)], 1)
+            top = jnp.concatenate([jnp.concatenate([bs[0], z8], 0), jnp.concatenate([bs[1], z8], 0)], 1)
             low = jnp.concatenate([jnp.concatenate([y0, z8], 0), jnp.concatenate([z8, y1], 0)], 1)
             rhs[p, 0:16, :] = top.astype(BF)
             rhs[p, 16:32, :] = low.astype(BF)
@@ -214,73 +210,92 @@
         rcopy(featx.at[2 * GRP + x], featx.at[2 * GRP + x], fz_send.at[0], f_recv.at[2 * GRP + x], (up, g)).wait_recv()
         project(2 * GRP + x)
 
-    zpad = jnp.zeros((96, 2 * BLK), BF)
+    zrow = jnp.zeros((16, 2 * BLK), BF)
     zbt = jnp.zeros((16, BLK), BF)
 
-    def stage_a(c, n, r, p, buf):
-        o = jnp.dot(lhs[c * PAIRS + r], jnp.concatenate([rhs[p], zpad], 0), preferred_element_type=F32)
+    def stage_a(c, n, r, p):
+        w, e = divmod(r, 8)
+        right = jnp.concatenate([rhs[p, 0:16, :], oneh[e]] + [zrow] * 6, 0)
+        h = jnp.dot(lp[2 * c + w], right, preferred_element_type=F32)
         nn = nf[n]
-        hb[buf, 0:BLK, :] = (o[:BLK] + jnp.concatenate([nn, nn], 1)).astype(BF)
-        hb[buf, BLK : 2 * BLK, :] = o[BLK:].astype(BF)
-
-    def stage_b(buf):
+        hb[r, 0:BLK, :] = (h + jnp.concatenate([nn, nn], 1)).astype(BF)
+        right = jnp.concatenate([zrow] * e + [rhs[p, 16:32, :]] + [zrow] * (7 - e), 0)
+        hb[r, BLK : 2 * BLK, :] = jnp.dot(lh[2 * c + w], right, preferred_element_type=F32).astype(BF)
+
+    def stage_b(r):
         for k in range(0, BLK, 16):
-            hid, pg = pair_values(hb[buf, k : k + 16, :], hb[buf, BLK + k : BLK + k + 16, :])
-            xb[buf, k : k + 16, :] = hid
-            xb[buf, BLK + k : BLK + k + 16, :] = pg
-
-    def stage_c(c, r, p, buf):
+            hid, pg = pair_values(hb[r, k : k + 16, :], hb[r, BLK + k : BLK + k + 16, :])
+            xb[r, k : k + 16, :] = hid
+            xb[r, BLK + k : BLK + k + 16, :] = pg
+
+    def stage_c(c, r, p):
         lr = jnp.concatenate([jnp.concatenate([bt[c * PAIRS + r], zbt], 1), wred[...]], 0)
-        o = jnp.dot(lr, xb[buf], preferred_element_type=F32)
+        o = jnp.dot(lr, xb[r], preferred_element_type=F32)
         for e in range(2):
+            i = 2 * r + e
             cut = slice(BLK * e, BLK * e + BLK)
-            al[2 * p + e] = o[8 * e : 8 * e + 8, cut]
-            pr[2 * p + e] = o[16:24, cut] * bas[2 * p + e]
-
-    def main(k, carry):
-        ta = jnp.minimum(k, NSLOT - 1)
-        tl = jnp.maximum(k - 1, 0)
-        ca, na, _, _ = slot_of(ta)
-        cl, _, _, _ = slot_of(tl)
-        for half in range(2):
-            for u in range(U):
-                r = half * U + u
-                stage_a(ca, na, r, ta * PAIRS + r, r)
-                stage_b((1 - half) * U + u)
-                stage_c(cl, r, tl * PAIRS + r, r)
-        return carry
-
-    lax.fori_loop(0, NSLOT + 1, main, 0)
-
-    def finish(t, carry):
+            al[8 * i : 8 * i + 8, :] = o[8 * e : 8 * e + 8, cut]
+            pr[8 * i : 8 * i + 8, :] = o[16:24, cut] * bas[2 * p + e]
+
+    def finish(t, ready):
         c, n, gs, ti = slot_of(t)
-        live = jnp.where(ti < meta_sm[gs, 0, 2 * SLOTS], 1.0, 0.0)
+        live = jnp.logical_and(ti < meta_sm[gs, 0, 2 * SLOTS], ready)
         ng = [jnp.zeros((8, BLK), F32)] * 3
-        base = t * QTR
         for q in range(QTR // 8):
             sl = slice(8 * q, 8 * q + 8)
-            at8 = pl.ds(base + 8 * q, 8)
-            s = pr[at8, 0, :]
+
+            def strip(ref, k):
+                return ref[pl.ds(64 * q + k, 8, stride=8), :]
+
+            s = strip(pr, 0)
             for b in range(1, 8):
-                s = s + pr[at8, b, :]
-            av = [al[at8, m, :] + al[at8, m + 4, :] for m in range(4)]
+                s = s + strip(pr, b)
+            av = [strip(al, m) + strip(al, m + 4) for m in range(4)]
             hd = [ds[t, k, sl, :] for k in range(3)]
             env = ds[t, 3, sl, :]
             ik = ds[t, 4, sl, :]
             eg = av[0] + av[1] * hd[0] + av[2] * hd[1] + av[3] * hd[2]
-            sq = (s - 0.5 * eg * ik) * (4.0 * live)
-            ev = env * (0.5 * live)
+            sq = (s - 0.5 * eg * ik) * 4.0
+            ev = env * 0.5
             for m in range(3):
-                dg = sq * hd[m] + ev * av[m + 1]
+                dg = jnp.where(live, sq * hd[m] + ev * av[m + 1], 0.0)
                 ng[m] = ng[m] + dg
                 for k in range(GRP):
                     cacc[k, m, sl, :] += jnp.where(c == k, 1.0, 0.0) * dg
         v = jnp.concatenate([jnp.sum(a, axis=0, keepdims=True) for a in ng] + [jnp.zeros((5, BLK), F32)], 0)
         for k in range(3 * GRP):
             nacc[k] += jnp.where(n == k, 1.0, 0.0) * v
+
+    def first(c):
+        return c[0], c[1]
+
+    ca, na = first(slot_of(0))
+    for r in range(PAIRS):
+        stage_a(ca, na, r, r)
+
+    def main(k, carry):
+        ca, na = first(slot_of(k))
+        tc = jnp.maximum(k - 2, 0)
+        cc, _ = first(slot_of(tc))
+        finish(jnp.maximum(k - 3, 0), k >= 3)
+        for r in range(PAIRS):
+            stage_c(cc, r, tc * PAIRS + r)
+            stage_b(r)
+            stage_a(ca, na, r, k * PAIRS + r)
         return carry
 
-    lax.fori_loop(0, NSLOT, finish, 0)
+    lax.fori_loop(1, NSLOT, main, 0)
+    last = NSLOT - 1
+    finish(last - 2, True)
+    cc, _ = first(slot_of(last - 1))
+    for r in range(PAIRS):
+        stage_c(cc, r, (last - 1) * PAIRS + r)
+        stage_b(r)
+    finish(last - 1, True)
+    cc, _ = first(slot_of(last))
+    for r in range(PAIRS):
+        stage_c(cc, r, last * PAIRS + r)
+    finish(last, True)
 
     crow = jnp.concatenate(
         [jnp.sum(cacc[:, m].reshape(BLK, BLK).T, axis=0, keepdims=True) for m in range(3)]
@@ -298,7 +313,8 @@
     for x in range(GRP):
         go(rcopy(res_send.at[x], res_recv.at[2 * GRP + g], r_send.at[3 + x], r_recv.at[2 * GRP + g], (dn, x)))
         go(rcopy(res_send.at[2 * GRP + x], res_recv.at[g], r_send.at[7 + x], r_recv.at[g], (up, x)))
-    total = res_send[own]
+    out_ref[0] = res_send[own][0:3, :]
+    total = jnp.zeros((8, BLK), F32)
     for x in xs:
         rcopy(res_recv.at[GRP + x], res_recv.at[GRP + x], r_send.at[0], r_recv.at[GRP + x], (dm, x)).wait_recv()
         total = total + res_recv[GRP + x]
@@ -309,19 +325,19 @@
             res_recv.at[2 * GRP + x], res_recv.at[2 * GRP + x], r_send.at[0], r_recv.at[2 * GRP + x], (up, x)
         ).wait_recv()
         total = total + res_recv[2 * GRP + x]
-    out_ref[...] = total[0:3, :]
+    out_ref[1] = total[0:3, :]
     for c in sends:
         c.wait_send()
 
 
-def on_device(*args):
+def on_device(pos, feat, nw, adj, bw, ew, tc, tn, cnt):
     V = pltpu.VMEM
     vs = pl.BlockSpec(memory_space=pltpu.VMEM)
     sm = pl.BlockSpec(memory_space=pltpu.SMEM)
     D = pltpu.SemaphoreType.DMA
-    return pl.pallas_call(
+    parts = pl.pallas_call(
         body,
-        out_shape=jax.ShapeDtypeStruct((3, BLK), F32),
+        out_shape=jax.ShapeDtypeStruct((2, 3, BLK), F32),
         in_specs=[vs] * 6 + [sm] * 3,
         out_specs=vs,
         scratch_shapes=[
@@ -338,19 +354,21 @@
             V((GRP, 3, QTR, BLK), F32),
             V((8 * BLK, BLK), F32),
             V((GRP * PAIRS, 16, BLK), BF),
-            V((GRP * PAIRS, 2 * BLK, BLK), BF),
+            V((2 * GRP, BLK, BLK), BF),
+            V((2 * GRP, BLK, BLK), BF),
+            V((8, 16, 2 * BLK), BF),
             V((16, 2 * BLK), BF),
             V((NSLOT * PAIRS, 32, 2 * BLK), BF),
             V((NSLOT * QTR, 8, BLK), F32),
-            V((NSLOT * QTR, 8, BLK), F32),
-            V((NSLOT * QTR, 8, BLK), F32),
+            V((8 * QTR, BLK), F32),
+            V((8 * QTR, BLK), F32),
             V((NSLOT, 5, QTR, BLK), F32),
             V((8 * QTR, BLK), F32),
             V((QTR, BLK), F32),
             V((3 * GRP, 8, BLK), F32),
             V((GRP, 3, QTR, BLK), F32),
-            V((2 * U, 2 * BLK, 2 * BLK), BF),
-            V((2 * U, 2 * BLK, 2 * BLK), BF),
+            V((PAIRS, 2 * BLK, 2 * BLK), BF),
+            V((PAIRS, 2 * BLK, 2 * BLK), BF),
             D((3,)),
             D((8,)),
             D((12,)),
@@ -366,7 +384,8 @@
         ],
         compiler_params=pltpu.CompilerParams(collective_id=0, has_side_effects=True),
         name="allegro_forces",
-    )(*args)
+    )(pos, feat, nw, adj, bw, ew.T, tc, tn, cnt)
+    return parts[0] + parts[1]
 
 
 def solution(mesh):

time: 55.7 us -> 51.1 us (0.917)
  the two profiles are of different devices: /device:TPU:1 before, /device:TPU:2 now
where the time goes in v2:
time: 51.1 us; the launch traced here: 50.9 us
  Pallas kernels  49 us (96%)
  other arithmetic  1.27 us (2%)
  between operations  0.66 us (1%)
    pallas_call x1, Pallas kernels, on_device(): pl.pallas_call(body, out_shape=jax.ShapeDtypeStruct((2, 3, BLK), F32), in...  49 us
    add x1, other arithmetic, on_device(): return parts[0] + parts[1]  1.27 us

profile of v2, /device:TPU:2, one launch (start us, length us, event | category | flops | bytes accessed | tf_op | source)
XLA Modules:
  0.0 50.9 jit_solution(904650404115967356)
XLA Ops:
  0.7 49.0 %allegro_forces.1 = f32[2,3,128]{2,1,0:T(4,128)} custom-call(f32[3,128]{1,0:T(4,128)} %pos_in.1, bf16[128,128]{1,0:T(8,128)(2,1)} %feat_in.1, bf16[128,128]{1,0:T(8,128)(2,1)} %nw_in.1, bf16[256,128]{1,0:T(8,128)(2,1)} %adj_in.1, bf16[8,128]{1,0:T(8,128)(2,1)} %bw_in.1, bf16[64,128]{1,0:T(8,128)(2,1)} %bitcast.3, s32[4]{0:T(128)} %tc_in.1, s32[4]{0:T(128)} %tn_in.1, ...), custom_call_target="tpu_custom_call" | custom-call | tf_op jit(solution)/shard_map/allegro_forces/pallas_call | solution.py:338
  49.6 1.3 %add_bitcast_fusion = f32[3,128]{1,0:T(4,128)} fusion(f32[2,3,128]{2,1,0:T(4,128)} %allegro_forces.1), kind=kLoop, calls=%fused_computation | loop fusion | flops 384 | bytes 4608 | tf_op jit(solution)/shard_map/add | solution.py:388

commit v3 on v2

--- a/solution.py
+++ b/solution.py
@@ -18,18 +18,18 @@
 RATES = tuple(0.3 * 1.5**b for b in range(8))
 
 
-def pair_values(h, hg):
+def pair_values(h):
     one = jnp.asarray(1.0, BF)
     t = jnp.tanh(h)
     p = one + t
     hid = h * p
-    return hid, hg * (p + hid * (one - t))
+    return hid, p + hid * (one - t)
 
 
 def body(
     pos_in, feat_in, nw_in, adj_in, bw_in, ew_in, tc_in, tn_in, cnt_in, out_ref,
     featx, posx, meta, meta_sm, at_send, at_all, res_send, res_recv,
-    nf, ptr, cposb, bt32, bt, lp, lh, oneh, wred, rhs, bas, al, pr, ds, y_s, s2_s, nacc, cacc,
+    nf, ptr, cposb, bt32, bmf, bt, wb, lp, oneh, rhs, bas, al, pr, ds, y_all, s2_s, nacc, cacc,
     hb, xb,
     fx_send, fz_send, f_recv, a_send, a_recv, p_send, p_recv, m_send, m_recv,
     r_send, r_recv, loc_sem,
@@ -87,13 +87,6 @@
 
     featx[own] = feat_in[...]
     at_all[g] = at_send[pl.ds(pl.multiple_of(QTR * g, QTR), QTR), :]
-    wred[...] = jnp.concatenate(
-        [
-            jnp.concatenate([jnp.zeros((8, BLK), F32), bw_in[...].astype(F32)], 1),
-            jnp.zeros((8, 2 * BLK), F32),
-        ],
-        0,
-    ).astype(BF)
     nacc[...] = jnp.zeros_like(nacc)
     cacc[...] = jnp.zeros_like(cacc)
 
@@ -107,6 +100,7 @@
         hi = bm.astype(BF).astype(F32)
         bt32[pl.ds(m, BLK, stride=8), :] = hi
         bt32[pl.ds(4 + m, BLK, stride=8), :] = bm - hi
+        bmf[BLK * m : BLK * m + BLK, :] = bm
 
     for j, x in enumerate((xs[0], xs[2], xs[1])):
         blk = GRP + x
@@ -123,9 +117,16 @@
         for w in range(2):
             f2 = pltpu.roll(fr, BLK - 16, 1) if w else fr
             lp[2 * c + w] = jnp.where(lane < 8, wt, jnp.where(lane < 16, 0.0, f2)).astype(BF)
-            lh[2 * c + w] = bt32[BLK * (2 * c + w) : BLK * (2 * c + w + 1), :].T.astype(BF)
-    for cp in range(GRP * PAIRS):
-        bt[cp] = bt32[16 * cp : 16 * cp + 16, :].astype(BF)
+    bwf = bw_in[...].astype(F32)
+
+    def centre_rows(cp, carry):
+        bt[cp] = bt32[pl.ds(pl.multiple_of(16 * cp, 16), 16), :].astype(BF)
+        for e in range(2):
+            v = [bmf[pl.ds(BLK * m + 2 * cp + e, 8, stride=0), :] * bwf for m in range(4)]
+            wb[cp, 32 * e : 32 * e + 32, :] = jnp.concatenate(v, 0).astype(BF)
+        return carry
+
+    lax.fori_loop(0, GRP * PAIRS, centre_rows, 0, unroll=8)
     row16 = lax.broadcasted_iota(jnp.int32, (16, 2 * BLK), 0)
     side = lax.broadcasted_iota(jnp.int32, (16, 2 * BLK), 1) // BLK
     for r in range(8):
@@ -177,8 +178,7 @@
             hd = [v * 0.5 for v in d]
             ys = [env] + [env * v for v in hd]
             for m in range(4):
-                y_s[pl.ds(64 * q + m, 8, stride=8), :] = ys[m]
-                y_s[pl.ds(64 * q + m + 4, 8, stride=8), :] = ys[m]
+                y_all[pl.ds(4 * QTR * t + 32 * q + m, 8, stride=4), :] = ys[m]
             for k, v in enumerate(hd + [env, inner * keep]):
                 ds[t, k, sl, :] = v
         for r in range(PAIRS):
@@ -188,12 +188,8 @@
                 b = jnp.exp(s2_s[pl.ds(2 * r + e, 8, stride=0), :] * neg)
                 bas[2 * p + e] = b * half_neg
                 bs.append(b)
-            y0 = y_s[16 * r : 16 * r + 8, :]
-            y1 = y_s[16 * r + 8 : 16 * r + 16, :]
             top = jnp.concatenate([jnp.concatenate([bs[0], z8], 0), jnp.concatenate([bs[1], z8], 0)], 1)
-            low = jnp.concatenate([jnp.concatenate([y0, z8], 0), jnp.concatenate([z8, y1], 0)], 1)
-            rhs[p, 0:16, :] = top.astype(BF)
-            rhs[p, 16:32, :] = low.astype(BF)
+            rhs[p] = top.astype(BF)
         return carry
 
     lax.fori_loop(0, NSLOT, geometry, 0)
@@ -215,27 +211,34 @@
 
     def stage_a(c, n, r, p):
         w, e = divmod(r, 8)
-        right = jnp.concatenate([rhs[p, 0:16, :], oneh[e]] + [zrow] * 6, 0)
+        right = jnp.concatenate([rhs[p], oneh[e]] + [zrow] * 6, 0)
         h = jnp.dot(lp[2 * c + w], right, preferred_element_type=F32)
         nn = nf[n]
-        hb[r, 0:BLK, :] = (h + jnp.concatenate([nn, nn], 1)).astype(BF)
-        right = jnp.concatenate([zrow] * e + [rhs[p, 16:32, :]] + [zrow] * (7 - e), 0)
-        hb[r, BLK : 2 * BLK, :] = jnp.dot(lh[2 * c + w], right, preferred_element_type=F32).astype(BF)
+        hb[r] = (h + jnp.concatenate([nn, nn], 1)).astype(BF)
 
     def stage_b(r):
         for k in range(0, BLK, 16):
-            hid, pg = pair_values(hb[r, k : k + 16, :], hb[r, BLK + k : BLK + k + 16, :])
+            hid, der = pair_values(hb[r, k : k + 16, :])
             xb[r, k : k + 16, :] = hid
-            xb[r, BLK + k : BLK + k + 16, :] = pg
+            xb[r, BLK + k : BLK + k + 16, :] = der
 
     def stage_c(c, r, p):
-        lr = jnp.concatenate([jnp.concatenate([bt[c * PAIRS + r], zbt], 1), wred[...]], 0)
+        cp = c * PAIRS + r
+        lr = jnp.concatenate(
+            [jnp.concatenate([bt[cp], zbt], 1), jnp.concatenate([jnp.zeros((64, BLK), BF), wb[cp]], 1)], 0
+        )
         o = jnp.dot(lr, xb[r], preferred_element_type=F32)
         for e in range(2):
             i = 2 * r + e
             cut = slice(BLK * e, BLK * e + BLK)
             al[8 * i : 8 * i + 8, :] = o[8 * e : 8 * e + 8, cut]
-            pr[8 * i : 8 * i + 8, :] = o[16:24, cut] * bas[2 * p + e]
+            first_row = 16 + 32 * e
+            v = None
+            for m in range(4):
+                ym = y_all[pl.ds(4 * (2 * p + e) + m, 8, stride=0), :]
+                w = ym * o[first_row + 8 * m : first_row + 8 * m + 8, cut]
+                v = w if v is None else v + w
+            pr[8 * i : 8 * i + 8, :] = v * bas[2 * p + e]
 
     def finish(t, ready):
         c, n, gs, ti = slot_of(t)
@@ -353,21 +356,21 @@
             V((BLK, BLK), F32),
             V((GRP, 3, QTR, BLK), F32),
             V((8 * BLK, BLK), F32),
+            V((4 * BLK, BLK), F32),
             V((GRP * PAIRS, 16, BLK), BF),
-            V((2 * GRP, BLK, BLK), BF),
+            V((GRP * PAIRS, 64, BLK), BF),
             V((2 * GRP, BLK, BLK), BF),
             V((8, 16, 2 * BLK), BF),
-            V((16, 2 * BLK), BF),
-            V((NSLOT * PAIRS, 32, 2 * BLK), BF),
+            V((NSLOT * PAIRS, 16, 2 * BLK), BF),
             V((NSLOT * QTR, 8, BLK), F32),
             V((8 * QTR, BLK), F32),
             V((8 * QTR, BLK), F32),
             V((NSLOT, 5, QTR, BLK), F32),
-            V((8 * QTR, BLK), F32),
+            V((4 * QTR * NSLOT, BLK), F32),
             V((QTR, BLK), F32),
             V((3 * GRP, 8, BLK), F32),
             V((GRP, 3, QTR, BLK), F32),
-            V((PAIRS, 2 * BLK, 2 * BLK), BF),
+            V((PAIRS, BLK, 2 * BLK), BF),
             V((PAIRS, 2 * BLK, 2 * BLK), BF),
             D((3,)),
             D((8,)),

time: 51.1 us -> 50.1 us (0.980)
  Pallas kernels: 49 us -> 48 us
    pallas_call x1, Pallas kernels: 49 us -> 48 us  [on_device(): pl.pallas_call(body, out_shape=jax.ShapeDtypeStruct((2, 3, BLK), F32), in...]
where the time goes in v3:
time: 50.1 us; the launch traced here: 49.9 us
  Pallas kernels  48 us (96%)
  other arithmetic  1.27 us (3%)
  between operations  0.66 us (1%)
    pallas_call x1, Pallas kernels, on_device(): pl.pallas_call(body, out_shape=jax.ShapeDtypeStruct((2, 3, BLK), F32), in...  48 us
    add x1, other arithmetic, on_device(): return parts[0] + parts[1]  1.27 us

profile of v3, /device:TPU:2, one launch (start us, length us, event | category | flops | bytes accessed | tf_op | source)
XLA Modules:
  0.0 49.9 jit_solution(8524888975091977777)
XLA Ops:
  0.7 48.0 %allegro_forces.1 = f32[2,3,128]{2,1,0:T(4,128)} custom-call(f32[3,128]{1,0:T(4,128)} %pos_in.1, bf16[128,128]{1,0:T(8,128)(2,1)} %feat_in.1, bf16[128,128]{1,0:T(8,128)(2,1)} %nw_in.1, bf16[256,128]{1,0:T(8,128)(2,1)} %adj_in.1, bf16[8,128]{1,0:T(8,128)(2,1)} %bw_in.1, bf16[64,128]{1,0:T(8,128)(2,1)} %bitcast.3, s32[4]{0:T(128)} %tc_in.1, s32[4]{0:T(128)} %tn_in.1, ...), custom_call_target="tpu_custom_call" | custom-call | tf_op jit(solution)/shard_map/allegro_forces/pallas_call | solution.py:341
  48.7 1.3 %add_bitcast_fusion = f32[3,128]{1,0:T(4,128)} fusion(f32[2,3,128]{2,1,0:T(4,128)} %allegro_forces.1), kind=kLoop, calls=%fused_computation | loop fusion | flops 384 | bytes 4608 | tf_op jit(solution)/shard_map/add | solution.py:391

commit v4 on v3

--- a/solution.py
+++ b/solution.py
@@ -27,9 +27,10 @@
 
 
 def body(
-    pos_in, feat_in, nw_in, adj_in, bw_in, ew_in, tc_in, tn_in, cnt_in, out_ref,
+    pos_h, feat_h, nw_h, adj_h, bw_h, ew_h, tc_h, tn_h, cnt_h, out_ref,
+    pos_in, feat_in, nw_in, adj_in, bw_in, ew_in, tc_in, tn_in, cnt_in, in_sem,
     featx, posx, meta, meta_sm, at_send, at_all, res_send, res_recv,
-    nf, ptr, cposb, bt32, bmf, bt, wb, lp, oneh, rhs, bas, al, pr, ds, y_all, s2_s, nacc, cacc,
+    nf, nwt, ptr, cposb, bt32, bmf, bt, wb, lp, oneh, eye2, rhs, bas, al, pr, ds, y_all, s2_s, nacc, cacc,
     hb, xb,
     fx_send, fz_send, f_recv, a_send, a_recv, p_send, p_recv, m_send, m_recv,
     r_send, r_recv, loc_sem,
@@ -39,6 +40,14 @@
     n_dom = lax.axis_size("dom")
     up = lax.rem(dm + 1, n_dom)
     dn = lax.rem(dm + n_dom - 1, n_dom)
+    pulls = [
+        pltpu.make_async_copy(src, dst, in_sem.at[i])
+        for i, (src, dst) in enumerate(
+            ((adj_h, adj_in), (nw_h, nw_in), (pos_h, pos_in), (tc_h, tc_in), (tn_h, tn_in), (cnt_h, cnt_in), (feat_h, feat_in), (bw_h, bw_in), (ew_h, ew_in))
+        )
+    ]
+    for c in pulls:
+        c.start()
     xs = [lax.rem(g + j, GRP) for j in range(1, GRP)]
     barrier = pltpu.get_barrier_semaphore()
     for x in xs:
@@ -49,6 +58,8 @@
 
     lane8 = lax.broadcasted_iota(jnp.int32, (8, BLK), 1)
     sub8 = lax.broadcasted_iota(jnp.int32, (8, BLK), 0)
+    for c in pulls[:6]:
+        c.wait()
     mv = jnp.zeros((8, BLK), jnp.int32)
     for t in range(SLOTS):
         mv = jnp.where(lane8 == t, tc_in[t], mv)
@@ -56,7 +67,28 @@
     meta[g] = jnp.where(lane8 == 2 * SLOTS, cnt_in[0], mv)
     posx[GRP + g] = jnp.concatenate([pos_in[...], jnp.zeros((5, BLK), F32)], 0)
     at_send[...] = adj_in[...].astype(F32).T.astype(BF)
-
+    nwt[...] = nw_in[...].astype(F32).T.astype(BF)
+
+    nacc[...] = jnp.zeros_like(nacc)
+    cacc[...] = jnp.zeros_like(cacc)
+    lane = lax.broadcasted_iota(jnp.int32, (BLK, BLK), 1)
+    eye = jnp.where(lane == lax.broadcasted_iota(jnp.int32, (BLK, BLK), 0), 1.0, 0.0).astype(BF)
+    eye2[...] = jnp.concatenate([eye, eye], 1)
+    row16 = lax.broadcasted_iota(jnp.int32, (16, 2 * BLK), 0)
+    side = lax.broadcasted_iota(jnp.int32, (16, 2 * BLK), 1) // BLK
+    for r in range(8):
+        oneh[r] = jnp.where(row16 == 2 * r + side, 1.0, 0.0).astype(BF)
+    for c in pulls[6:]:
+        c.wait()
+    bwf = bw_in[...].astype(F32)
+    own = GRP + g
+    featx[own] = feat_in[...]
+
+    def project(b):
+        v = jnp.dot(nwt[...], featx[b], preferred_element_type=F32)
+        nf[b] = (v.astype(BF).astype(F32) * 0.5).astype(BF)
+
+    project(own)
     pl.semaphore_wait(barrier, 11)
 
     def rcopy(src, dst, ss, rs, dev):
@@ -70,7 +102,6 @@
         c.start()
         sends.append(c)
 
-    own = GRP + g
     for j, x in enumerate(xs):
         go(rcopy(posx.at[own], posx.at[own], p_send.at[j], p_recv.at[own], (dm, x)))
         go(rcopy(meta.at[g], meta.at[g], m_send.at[j], m_recv.at[g], (dm, x)))
@@ -85,10 +116,7 @@
     go(rcopy(feat_in, featx.at[g], fz_send.at[0], f_recv.at[g], (up, g)))
     go(rcopy(feat_in, featx.at[2 * GRP + g], fz_send.at[1], f_recv.at[2 * GRP + g], (dn, g)))
 
-    featx[own] = feat_in[...]
     at_all[g] = at_send[pl.ds(pl.multiple_of(QTR * g, QTR), QTR), :]
-    nacc[...] = jnp.zeros_like(nacc)
-    cacc[...] = jnp.zeros_like(cacc)
 
     for x in xs:
         rcopy(at_all.at[x], at_all.at[x], a_send.at[0], a_recv.at[x], (dm, x)).wait_recv()
@@ -108,16 +136,14 @@
         go(rcopy(featx.at[blk], featx.at[x], fz_send.at[2 + 2 * j], f_recv.at[x], (up, g)))
         go(rcopy(featx.at[blk], featx.at[2 * GRP + x], fz_send.at[3 + 2 * j], f_recv.at[2 * GRP + x], (dn, g)))
 
-    lane = lax.broadcasted_iota(jnp.int32, (BLK, BLK), 1)
     wt = (
-        jnp.concatenate([bw_in[...].astype(F32), jnp.zeros((BLK - 8, BLK), F32)], 0).T * 0.5
+        jnp.concatenate([bwf, jnp.zeros((BLK - 8, BLK), F32)], 0).T * 0.5
     )
     for c in range(GRP):
         fr = pltpu.roll(featx[GRP + c].astype(F32) * 0.5, lax.rem(16 + BLK - QTR * g, BLK), 1)
         for w in range(2):
             f2 = pltpu.roll(fr, BLK - 16, 1) if w else fr
             lp[2 * c + w] = jnp.where(lane < 8, wt, jnp.where(lane < 16, 0.0, f2)).astype(BF)
-    bwf = bw_in[...].astype(F32)
 
     def centre_rows(cp, carry):
         bt[cp] = bt32[pl.ds(pl.multiple_of(16 * cp, 16), 16), :].astype(BF)
@@ -127,11 +153,6 @@
         return carry
 
     lax.fori_loop(0, GRP * PAIRS, centre_rows, 0, unroll=8)
-    row16 = lax.broadcasted_iota(jnp.int32, (16, 2 * BLK), 0)
-    side = lax.broadcasted_iota(jnp.int32, (16, 2 * BLK), 1) // BLK
-    for r in range(8):
-        oneh[r] = jnp.where(row16 == 2 * r + side, 1.0, 0.0).astype(BF)
-
     for x in xs:
         rcopy(posx.at[GRP + x], posx.at[GRP + x], p_send.at[0], p_recv.at[GRP + x], (dm, x)).wait_recv()
         rcopy(meta.at[x], meta.at[x], m_send.at[0], m_recv.at[x], (dm, x)).wait_recv()
@@ -194,12 +215,8 @@
 
     lax.fori_loop(0, NSLOT, geometry, 0)
 
-    def project(b):
-        v = lax.dot_general(nw_in[...], featx[b], (((0,), (0,)), ((), ())), preferred_element_type=F32)
-        nf[b] = v.astype(BF).astype(F32) * 0.5
-
-    for c in range(GRP):
-        project(GRP + c)
+    for x in xs:
+        project(GRP + x)
     for x in [g, *xs]:
         rcopy(featx.at[x], featx.at[x], fz_send.at[0], f_recv.at[x], (dn, g)).wait_recv()
         project(x)
@@ -209,38 +226,37 @@
     zrow = jnp.zeros((16, 2 * BLK), BF)
     zbt = jnp.zeros((16, BLK), BF)
 
-    def stage_a(c, n, r, p):
+    def stage_a(b, c, n, r, p):
         w, e = divmod(r, 8)
-        right = jnp.concatenate([rhs[p], oneh[e]] + [zrow] * 6, 0)
-        h = jnp.dot(lp[2 * c + w], right, preferred_element_type=F32)
-        nn = nf[n]
-        hb[r] = (h + jnp.concatenate([nn, nn], 1)).astype(BF)
-
-    def stage_b(r):
+        right = jnp.concatenate([eye2[...], rhs[p], oneh[e]] + [zrow] * 6, 0)
+        left = jnp.concatenate([nf[n], lp[2 * c + w]], 1)
+        hb[b, r] = jnp.dot(left, right, preferred_element_type=F32).astype(BF)
+
+    def stage_b(b, r):
         for k in range(0, BLK, 16):
-            hid, der = pair_values(hb[r, k : k + 16, :])
-            xb[r, k : k + 16, :] = hid
-            xb[r, BLK + k : BLK + k + 16, :] = der
-
-    def stage_c(c, r, p):
+            hid, der = pair_values(hb[b, r, k : k + 16, :])
+            xb[b, r, k : k + 16, :] = hid
+            xb[b, r, BLK + k : BLK + k + 16, :] = der
+
+    def stage_c(b, c, r, p):
         cp = c * PAIRS + r
         lr = jnp.concatenate(
             [jnp.concatenate([bt[cp], zbt], 1), jnp.concatenate([jnp.zeros((64, BLK), BF), wb[cp]], 1)], 0
         )
-        o = jnp.dot(lr, xb[r], preferred_element_type=F32)
+        o = jnp.dot(lr, xb[b, r], preferred_element_type=F32)
         for e in range(2):
             i = 2 * r + e
             cut = slice(BLK * e, BLK * e + BLK)
-            al[8 * i : 8 * i + 8, :] = o[8 * e : 8 * e + 8, cut]
+            al[b, 8 * i : 8 * i + 8, :] = o[8 * e : 8 * e + 8, cut]
             first_row = 16 + 32 * e
             v = None
             for m in range(4):
                 ym = y_all[pl.ds(4 * (2 * p + e) + m, 8, stride=0), :]
                 w = ym * o[first_row + 8 * m : first_row + 8 * m + 8, cut]
                 v = w if v is None else v + w
-            pr[8 * i : 8 * i + 8, :] = v * bas[2 * p + e]
-
-    def finish(t, ready):
+            pr[b, 8 * i : 8 * i + 8, :] = v * bas[2 * p + e]
+
+    def finish(b, t, ready):
         c, n, gs, ti = slot_of(t)
         live = jnp.logical_and(ti < meta_sm[gs, 0, 2 * SLOTS], ready)
         ng = [jnp.zeros((8, BLK), F32)] * 3
@@ -248,11 +264,11 @@
             sl = slice(8 * q, 8 * q + 8)
 
             def strip(ref, k):
-                return ref[pl.ds(64 * q + k, 8, stride=8), :]
+                return ref[b, pl.ds(64 * q + k, 8, stride=8), :]
 
             s = strip(pr, 0)
-            for b in range(1, 8):
-                s = s + strip(pr, b)
+            for j in range(1, 8):
+                s = s + strip(pr, j)
             av = [strip(al, m) + strip(al, m + 4) for m in range(4)]
             hd = [ds[t, k, sl, :] for k in range(3)]
             env = ds[t, 3, sl, :]
@@ -272,33 +288,34 @@
     def first(c):
         return c[0], c[1]
 
+    def step(k, par, do_a, do_b):
+        one = 1 - par
+        finish(one, jnp.maximum(k - 3, 0), k >= 3)
+        tc = jnp.maximum(k - 2, 0)
+        cc, _ = first(slot_of(tc))
+        if do_a:
+            ca, na = first(slot_of(k))
+        for r in range(PAIRS):
+            stage_c(par, cc, r, tc * PAIRS + r)
+            if do_b:
+                stage_b(one, r)
+            if do_a:
+                stage_a(par, ca, na, r, k * PAIRS + r)
+
     ca, na = first(slot_of(0))
     for r in range(PAIRS):
-        stage_a(ca, na, r, r)
-
-    def main(k, carry):
-        ca, na = first(slot_of(k))
-        tc = jnp.maximum(k - 2, 0)
-        cc, _ = first(slot_of(tc))
-        finish(jnp.maximum(k - 3, 0), k >= 3)
-        for r in range(PAIRS):
-            stage_c(cc, r, tc * PAIRS + r)
-            stage_b(r)
-            stage_a(ca, na, r, k * PAIRS + r)
+        stage_a(0, ca, na, r, r)
+
+    def main(j, carry):
+        step(2 * j + 1, 1, True, True)
+        step(2 * j + 2, 0, True, True)
         return carry
 
-    lax.fori_loop(1, NSLOT, main, 0)
-    last = NSLOT - 1
-    finish(last - 2, True)
-    cc, _ = first(slot_of(last - 1))
-    for r in range(PAIRS):
-        stage_c(cc, r, (last - 1) * PAIRS + r)
-        stage_b(r)
-    finish(last - 1, True)
-    cc, _ = first(slot_of(last))
-    for r in range(PAIRS):
-        stage_c(cc, r, last * PAIRS + r)
-    finish(last, True)
+    lax.fori_loop(0, NSLOT // 2 - 1, main, 0)
+    step(NSLOT - 1, 1, True, True)
+    step(NSLOT, 0, False, True)
+    step(NSLOT + 1, 1, False, False)
+    finish(1, NSLOT - 1, True)
 
     crow = jnp.concatenate(
         [jnp.sum(cacc[:, m].reshape(BLK, BLK).T, axis=0, keepdims=True) for m in range(3)]
@@ -336,14 +353,24 @@
 def on_device(pos, feat, nw, adj, bw, ew, tc, tn, cnt):
     V = pltpu.VMEM
     vs = pl.BlockSpec(memory_space=pltpu.VMEM)
-    sm = pl.BlockSpec(memory_space=pltpu.SMEM)
+    hb = pl.BlockSpec(memory_space=pl.ANY)
     D = pltpu.SemaphoreType.DMA
     parts = pl.pallas_call(
         body,
         out_shape=jax.ShapeDtypeStruct((2, 3, BLK), F32),
-        in_specs=[vs] * 6 + [sm] * 3,
+        in_specs=[hb] * 9,
         out_specs=vs,
         scratch_shapes=[
+            V((3, BLK), F32),
+            V((BLK, BLK), BF),
+            V((BLK, BLK), BF),
+            V((2 * BLK, BLK), BF),
+            V((8, BLK), BF),
+            V((64, BLK), BF),
+            pltpu.SMEM((SLOTS,), jnp.int32),
+            pltpu.SMEM((SLOTS,), jnp.int32),
+            pltpu.SMEM((1,), jnp.int32),
+            D((9,)),
             V((3 * GRP, BLK, BLK), BF),
             V((3 * GRP, 8, BLK), F32),
             V((GRP, 8, BLK), jnp.int32),
@@ -352,7 +379,8 @@
             V((GRP, QTR, 256), BF),
             V((3 * GRP, 8, BLK), F32),
             V((3 * GRP, 8, BLK), F32),
-            V((3 * GRP, BLK, BLK), F32),
+            V((3 * GRP, BLK, BLK), BF),
+            V((BLK, BLK), BF),
             V((BLK, BLK), F32),
             V((GRP, 3, QTR, BLK), F32),
             V((8 * BLK, BLK), F32),
@@ -361,17 +389,18 @@
             V((GRP * PAIRS, 64, BLK), BF),
             V((2 * GRP, BLK, BLK), BF),
             V((8, 16, 2 * BLK), BF),
+            V((BLK, 2 * BLK), BF),
             V((NSLOT * PAIRS, 16, 2 * BLK), BF),
             V((NSLOT * QTR, 8, BLK), F32),
-            V((8 * QTR, BLK), F32),
-            V((8 * QTR, BLK), F32),
+            V((2, 8 * QTR, BLK), F32),
+            V((2, 8 * QTR, BLK), F32),
             V((NSLOT, 5, QTR, BLK), F32),
             V((4 * QTR * NSLOT, BLK), F32),
             V((QTR, BLK), F32),
             V((3 * GRP, 8, BLK), F32),
             V((GRP, 3, QTR, BLK), F32),
-            V((PAIRS, BLK, 2 * BLK), BF),
-            V((PAIRS, 2 * BLK, 2 * BLK), BF),
+            V((2, PAIRS, BLK, 2 * BLK), BF),
+            V((2, PAIRS, 2 * BLK, 2 * BLK), BF),
             D((3,)),
             D((8,)),
             D((12,)),

time: 50.1 us -> 47.6 us (0.950)
  Pallas kernels: 48 us -> 45.5 us
    pallas_call x1, Pallas kernels: 48 us -> 45.5 us  [on_device(): pl.pallas_call(body, out_shape=jax.ShapeDtypeStruct((2, 3, BLK), F32), in...]
where the time goes in v4:
time: 47.6 us; the launch traced here: 47.4 us
  Pallas kernels  45.5 us (96%)
  other arithmetic  1.27 us (3%)
  between operations  0.66 us (1%)
    pallas_call x1, Pallas kernels, on_device(): pl.pallas_call(body, out_shape=jax.ShapeDtypeStruct((2, 3, BLK), F32), in...  45.5 us
    add x1, other arithmetic, on_device(): return parts[0] + parts[1]  1.27 us

profile of v4, /device:TPU:2, one launch (start us, length us, event | category | flops | bytes accessed | tf_op | source)
XLA Modules:
  0.0 47.4 jit_solution(14900711863352088583)
XLA Ops:
  0.7 45.5 %allegro_forces.1 = f32[2,3,128]{2,1,0:T(4,128)} custom-call(f32[3,128]{1,0:T(4,128)} %pos_h.1, bf16[128,128]{1,0:T(8,128)(2,1)} %feat_h.1, bf16[128,128]{1,0:T(8,128)(2,1)} %nw_h.1, bf16[256,128]{1,0:T(8,128)(2,1)} %adj_h.1, bf16[8,128]{1,0:T(8,128)(2,1)} %bw_h.1, bf16[64,128]{1,0:T(8,128)(2,1)} %bitcast.3, s32[4]{0:T(128)} %tc_h.1, s32[4]{0:T(128)} %tn_h.1, ...), custom_call_target="tpu_custom_call" | custom-call | tf_op jit(solution)/shard_map/allegro_forces/pallas_call | solution.py:358
  46.2 1.3 %add_bitcast_fusion = f32[3,128]{1,0:T(4,128)} fusion(f32[2,3,128]{2,1,0:T(4,128)} %allegro_forces.1), kind=kLoop, calls=%fused_computation | loop fusion | flops 384 | bytes 4608 | tf_op jit(solution)/shard_map/add | solution.py:420
